TPU v7x, 32 devices: a whole 2x2x4 slice. The times are simulated.
32 devices in a mesh: dp: 4 (over y, x), tensor: 8 (over z, core).
Axes of the slice: x: 2, y: 2, z: 4, core: 2. Of those that a mesh axis runs over, the one named last changes fastest.
Arguments:
- block_in: bfloat16 [8192, 1024], P(('dp', 'tensor')), may hold values from -10 to 10
- cotangent: bfloat16 [8192, 1024], P(('dp', 'tensor')), may hold values from -6 to 6
- lengths: int32 [16], P('dp'), may hold values from 1 to 512, as said below
- qkv_weight: float32 [3, 1024, 1024], P(None, 'dp', 'tensor'), may hold values from -0.1875 to 0.1875
- proj_weight: float32 [1024, 1024], P('tensor', 'dp'), may hold values from -0.75 to 0.75
- expand_weight: float32 [1024, 4096], P('dp', 'tensor'), may hold values from -0.1875 to 0.1875
- reduce_weight: float32 [4096, 1024], P('tensor', 'dp'), may hold values from -0.09375 to 0.09375
- split_bias: float32 [16, 384], P('tensor', 'dp'), may hold values from -0.6 to 0.6
- vector_params: float32 [6, 1024], P(None, 'dp'), may hold values from -0.6 to 0.6
- qkv_moments: float32 [2, 3, 1024, 1024], P(None, None, 'dp', 'tensor'), may hold values from -3 to 3, as said below
- proj_moments: float32 [2, 1024, 1024], P(None, 'tensor', 'dp'), may hold values from -3 to 3, as said below
- expand_moments: float32 [2, 1024, 4096], P(None, 'dp', 'tensor'), may hold values from -3 to 3, as said below
- reduce_moments: float32 [2, 4096, 1024], P(None, 'tensor', 'dp'), may hold values from -3 to 3, as said below
- bias_moments: float32 [2, 16, 384], P(None, 'tensor', 'dp'), may hold values from -3 to 3, as said below
- vector_moments: float32 [2, 6, 1024], P(None, None, 'dp'), may hold values from -3 to 3, as said below
Outputs:
- block_out: bfloat16 [8192, 1024], P(('dp', 'tensor'))
- input_grad: bfloat16 [8192, 1024], P(('dp', 'tensor'))
- qkv_grad: float32 [3, 1024, 1024], P(None, 'dp', 'tensor')
- proj_grad: float32 [1024, 1024], P('tensor', 'dp')
- expand_grad: float32 [1024, 4096], P('dp', 'tensor')
- reduce_grad: float32 [4096, 1024], P('tensor', 'dp')
- bias_grad: float32 [16, 384], P('tensor', 'dp')
- vector_grad: float32 [6, 1024], P(None, 'dp')
- qkv_new: float32 [3, 1024, 1024], P(None, 'dp', 'tensor')
- proj_new: float32 [1024, 1024], P('tensor', 'dp')
- expand_new: float32 [1024, 4096], P('dp', 'tensor')
- reduce_new: float32 [4096, 1024], P('tensor', 'dp')
- bias_new: float32 [16, 384], P('tensor', 'dp')
- vector_new: float32 [6, 1024], P(None, 'dp')
- qkv_state: float32 [2, 3, 1024, 1024], P(None, None, 'dp', 'tensor')
- proj_state: float32 [2, 1024, 1024], P(None, 'tensor', 'dp')
- expand_state: float32 [2, 1024, 4096], P(None, 'dp', 'tensor')
- reduce_state: float32 [2, 4096, 1024], P(None, 'tensor', 'dp')
- bias_state: float32 [2, 16, 384], P(None, 'tensor', 'dp')
- vector_state: float32 [2, 6, 1024], P(None, None, 'dp')
Inputs may be any that keep to these rules, and one draw needn't show every extreme that they name: `lengths`: sequence s lies on the dp member s // (number of sequences per dp member); every draw has a sequence of exactly 512 live slots. `qkv_moments`: index 0 holds first moments, index 1 second moments of at least 0.01. `proj_moments`: index 0 holds first moments, index 1 second moments of at least 0.01. `expand_moments`: index 0 holds first moments, index 1 second moments of at least 0.01. `reduce_moments`: index 0 holds first moments, index 1 second moments of at least 0.01. `bias_moments`: index 0 holds first moments, index 1 second moments of at least 0.01. `vector_moments`: index 0 holds first moments, index 1 second moments of at least 0.01.
All inputs are finite; a program needn't handle non-finite values.
Results may differ from a plain program's by a relative error of at most 0.025.
Values may be sent and summed in bfloat16 or wider, within the bound.
No kernel may reach another device: no remote copies, remote signals or barrier semaphores. Data moves between devices by JAX's collectives and lax.ppermute only.
A program may use at most 192 MiB of HBM per device.

v0:
```python
import functools

import jax
import jax.numpy as jnp
from jax import lax
from jax.experimental import pallas as pl
from jax.experimental.pallas import tpu as pltpu
from jax.sharding import Mesh
from jax.sharding import PartitionSpec as P


L = 512
STEP = 10
HD = 64
LANES = 128
GRANT = 20 << 20


norm_eps = 1e-05
beta_one = 0.9
beta_two = 0.999
learn_rate = 0.02
decay_rate = 0.01
adam_eps = 1e-08
half = jnp.bfloat16
single = jnp.float32


def gelu_pair(before):
    cumul = 0.5 * (1.0 + lax.erf(before * 0.7071067811865476))
    density = jnp.exp(-0.5 * before * before) * 0.3989422804014327
    return (before * cumul, cumul + before * density)


def adamw_step(weight, moments, grad, decay):
    first_one = lax.broadcasted_iota(jnp.int32, moments.shape, 0) == 0
    state = jnp.where(
        first_one,
        beta_one * moments + (1.0 - beta_one) * grad,
        beta_two * moments + (1.0 - beta_two) * grad * grad,
    )
    first = beta_one * moments[0] + (1.0 - beta_one) * grad
    second = beta_two * moments[1] + (1.0 - beta_two) * grad * grad
    scale_one = 1.0 - beta_one**STEP
    scale_two = 1.0 - beta_two**STEP
    update = first / scale_one / (jnp.sqrt(second / scale_two) + adam_eps) + decay * weight
    return (weight - learn_rate * update, state)


def dot(a, b, dims, kind=single):
    return lax.dot_general(a, b, (dims, ((), ())), preferred_element_type=single).astype(kind)


def call(kernel, **options):
    params = pltpu.CompilerParams(vmem_limit_bytes=GRANT)
    return pl.pallas_call(kernel, compiler_params=params, **options)


NN = ((1,), (0,))
NT = ((1,), (1,))
TN = ((0,), (0,))


def attend_kernel(q_ref, k_ref, v_ref, mask_ref, out_ref, lse_ref):
    lane = lax.broadcasted_iota(jnp.int32, (1, LANES), 1)
    q, k, v = q_ref[...], k_ref[...], v_ref[...]
    out = lse = None
    for head in range(LANES // HD):
        mine = (lane >= head * HD) & (lane < (head + 1) * HD)
        q_h = jnp.where(mine, q, jnp.zeros_like(q))
        scores = dot(q_h, k, NT) * HD ** (-0.5) + mask_ref[...]
        row_max = jnp.max(scores, axis=-1, keepdims=True)
        exponent = jnp.exp(scores - row_max)
        total = jnp.sum(exponent, axis=-1, keepdims=True)
        prob = (exponent / total).astype(half)
        out_h = dot(prob, v, NN)
        lse_h = jnp.broadcast_to(row_max + jnp.log(total), out_h.shape)
        out = out_h if out is None else jnp.where(mine, out_h, out)
        lse = lse_h if lse is None else jnp.where(mine, lse_h, lse)
    out_ref[...] = out.astype(half)
    lse_ref[...] = lse


def group_block(j, per):
    return lambda i: (0, (i // per) * 4 * per + j * per + i % per)


def attend(projected, mask, per):
    rows, width = projected.shape
    blocks = width // (4 * LANES)
    block = (rows, LANES)
    return call(
        attend_kernel,
        grid=(blocks,),
        in_specs=[pl.BlockSpec(block, group_block(j, per)) for j in range(3)]
        + [pl.BlockSpec((1, rows), lambda i: (0, 0))],
        out_specs=[pl.BlockSpec(block, lambda i: (0, i))] * 2,
        out_shape=[
            jax.ShapeDtypeStruct((rows, width // 4), half),
            jax.ShapeDtypeStruct((rows, width // 4), single),
        ],
        cost_estimate=pl.CostEstimate(
            flops=blocks * 8 * rows * rows * LANES,
            bytes_accessed=rows * width * 4,
            transcendentals=blocks * 2 * rows * rows,
        ),
    )(projected, projected, projected, mask)


def attend_back_kernel(per, q_ref, k_ref, v_ref, up_ref, lse_ref, mask_ref, out_ref, sum_ref):
    block = pl.program_id(0)
    lane = lax.broadcasted_iota(jnp.int32, (1, LANES), 1)
    q, k, v, up = q_ref[...], k_ref[...], v_ref[...], up_ref[...]
    grads = None
    for head in range(LANES // HD):
        mine = (lane >= head * HD) & (lane < (head + 1) * HD)
        q_h = jnp.where(mine, q, jnp.zeros_like(q))
        up_h = jnp.where(mine, up, jnp.zeros_like(up))
        scores = dot(q_h, k, NT) * HD ** (-0.5) + mask_ref[...]
        prob = jnp.exp(scores - lse_ref[:, head * HD : head * HD + 1])
        d_prob = dot(up_h, v, NT)
        delta = jnp.sum(prob * d_prob, axis=-1, keepdims=True)
        d_score = (prob * (d_prob - delta) * HD ** (-0.5)).astype(half)
        now = (dot(d_score, k, NN), dot(d_score, q, TN), dot(prob.astype(half), up, TN))
        grads = now if grads is None else [jnp.where(mine, a, b) for a, b in zip(now, grads)]
    parts = [g.astype(half) for g in grads] + [jnp.zeros_like(q)]
    for j in range(4):
        start = ((block // per) * 4 * per + j * per + block % per) * LANES
        out_ref[:, pl.ds(pl.multiple_of(start, LANES), LANES)] = parts[j]
    row = lax.broadcasted_iota(jnp.int32, (8, LANES), 0)
    for j, grad in enumerate((grads[0], None, grads[2], None)):
        start = ((block // per) * 4 * per + j * per + block % per) * LANES
        total = 0.0 if grad is None else jnp.sum(grad, axis=0, keepdims=True)
        sums = jnp.where(row == 6, total, 0.0)
        sum_ref[:, pl.ds(pl.multiple_of(start, LANES), LANES)] = sums


def attend_back(projected, upstream, lse, mask, per):
    rows, width = projected.shape
    blocks = width // (4 * LANES)
    block = (rows, LANES)
    return call(
        functools.partial(attend_back_kernel, per),
        grid=(blocks,),
        in_specs=[pl.BlockSpec(block, group_block(j, per)) for j in range(3)]
        + [
            pl.BlockSpec(block, lambda i: (0, i)),
            pl.BlockSpec(block, lambda i: (0, i)),
            pl.BlockSpec((1, rows), lambda i: (0, 0)),
        ],
        out_specs=[
            pl.BlockSpec((rows, width), lambda i: (0, 0)),
            pl.BlockSpec((8, width), lambda i: (0, 0)),
        ],
        out_shape=[
            jax.ShapeDtypeStruct((rows, width), half),
            jax.ShapeDtypeStruct((8, width), single),
        ],
        cost_estimate=pl.CostEstimate(
            flops=blocks * 20 * rows * rows * LANES,
            bytes_accessed=rows * width * 6,
            transcendentals=blocks * 2 * rows * rows,
        ),
    )(projected, projected, projected, upstream, lse, mask)


def normal_rows(resid):
    center = resid - jnp.mean(resid, axis=-1, keepdims=True)
    inv_std = lax.rsqrt(jnp.mean(center * center, axis=-1, keepdims=True) + norm_eps)
    return center * inv_std, inv_std


def norm_back(scaled, normed, inv_std):
    return inv_std * (
        scaled
        - jnp.mean(scaled, axis=-1, keepdims=True)
        - normed * jnp.mean(scaled * normed, axis=-1, keepdims=True)
    )


def first_norm_kernel(x_ref, mine_ref, other_ref, vec_ref, hidden_ref, half_ref, normed_ref, inv_ref):
    attn = mine_ref[...].astype(single) + other_ref[...].astype(single)
    resid = x_ref[...].astype(single) + attn + vec_ref[0:1, :]
    normed, inv_std = normal_rows(resid)
    hidden = normed * (1.0 + vec_ref[1:2, :]) + vec_ref[2:3, :]
    hidden_ref[...] = hidden
    half_ref[...] = hidden.astype(half)
    normed_ref[...] = normed
    inv_ref[...] = jnp.broadcast_to(inv_std, inv_ref.shape)


def add_sums(sum_ref, start, terms):
    row = lax.broadcasted_iota(jnp.int32, sum_ref.shape, 0)
    now = jnp.zeros(sum_ref.shape, single)
    for i, term in enumerate(terms):
        total = jnp.sum(term, axis=0, keepdims=True)
        now = now + jnp.where(row == start + i, total, 0.0)

    @pl.when(pl.program_id(0) == 0)
    def _():
        sum_ref[...] = now

    @pl.when(pl.program_id(0) != 0)
    def _():
        sum_ref[...] += now


def second_norm_kernel(
    hidden_ref, mine_ref, other_ref, up_ref, live_ref, vec_ref, out_ref, two_ref, half_ref, sum_ref
):
    ffn = mine_ref[...].astype(single) + other_ref[...].astype(single)
    resid = hidden_ref[...] + ffn + vec_ref[3:4, :]
    normed, inv_std = normal_rows(resid)
    gain = 1.0 + vec_ref[4:5, :]
    out_ref[...] = (normed * gain + vec_ref[5:6, :]).astype(half)
    grad_out = jnp.where(live_ref[:, 0:1] > 0.0, up_ref[...].astype(single), 0.0)
    d_two = norm_back(grad_out * gain, normed, inv_std)
    two_ref[...] = d_two
    half_ref[...] = d_two.astype(half)
    add_sums(sum_ref, 3, [d_two, grad_out * normed, grad_out])


def first_back_kernel(
    two_ref, mine_ref, other_ref, normed_ref, inv_ref, vec_ref, one_ref, half_ref, sum_ref
):
    term = mine_ref[...].astype(single) + other_ref[...].astype(single)
    d_hidden = two_ref[...] + term
    normed = normed_ref[...]
    d_one = norm_back(d_hidden * (1.0 + vec_ref[1:2, :]), normed, inv_ref[:, 0:1])
    one_ref[...] = d_one
    half_ref[...] = d_one.astype(half)
    add_sums(sum_ref, 0, [d_one, d_hidden * normed, d_hidden])


def by_rows(kernel, inputs, outputs, sums):
    rows = inputs[0].shape[0]
    tile = min(rows, 128)

    def spec(shape):
        if shape[0] == rows:
            return pl.BlockSpec((tile, shape[1]), lambda i: (i, 0))
        return pl.BlockSpec(shape, lambda i: (0, 0))

    shapes = [jax.ShapeDtypeStruct((rows, w), kind) for w, kind in outputs]
    shapes += [jax.ShapeDtypeStruct((8, sums), single)] if sums else []
    return call(
        kernel,
        grid=(rows // tile,),
        in_specs=[spec(a.shape) for a in inputs],
        out_specs=[spec(a.shape) for a in shapes],
        out_shape=shapes,
        cost_estimate=pl.CostEstimate(
            flops=40 * rows * inputs[0].shape[1],
            bytes_accessed=20 * rows * inputs[0].shape[1],
            transcendentals=rows,
        ),
    )(*inputs)


def first_grad_kernel(
    size, per, x_ref, stack_ref, one_ref, heads_ref, vec_ref, qv_ref, unit_ref, out_ref
):
    out_ref[0:size, :] = dot(x_ref[...], stack_ref[...], TN, half)
    proj = dot(one_ref[...], heads_ref[...], TN, half)
    span = per * LANES
    for g in range(proj.shape[1] // span):
        start = (4 * g + 3) * span
        out_ref[0:size, start : start + span] = proj[:, g * span : (g + 1) * span]
    small = vec_ref[...] + qv_ref[...] + unit_ref[...]
    blank = jnp.zeros((out_ref.shape[0] - size - 8, small.shape[1]), single)
    out_ref[size:, :] = jnp.concatenate([small, blank], 0).astype(half)


def first_grad(x, stack, one, heads, vec, qv, unit, wanted, size, per, extra):
    rows, width = stack.shape
    first, stride = wanted[0], (wanted[1] - wanted[0] if len(wanted) > 1 else 1)
    assert wanted == [first + i * stride for i in range(len(wanted))]
    return call(
        functools.partial(first_grad_kernel, size, per),
        grid=(len(wanted),),
        in_specs=[
            pl.BlockSpec((rows, size), lambda i: (0, first + i * stride)),
            pl.BlockSpec(stack.shape, lambda i: (0, 0)),
            pl.BlockSpec((rows, size), lambda i: (0, first + i * stride)),
            pl.BlockSpec(heads.shape, lambda i: (0, 0)),
            pl.BlockSpec((8, width), lambda i: (0, first + i * stride)),
            whole_spec(qv.shape),
            whole_spec(unit.shape),
        ],
        out_specs=pl.BlockSpec((size + extra, width), lambda i: (i, 0)),
        out_shape=jax.ShapeDtypeStruct((len(wanted) * (size + extra), width), half),
        cost_estimate=pl.CostEstimate(
            flops=len(wanted) * 2 * rows * size * (width + heads.shape[1]),
            bytes_accessed=rows * width * 4,
            transcendentals=0,
        ),
    )(x, stack, one, heads, vec, qv, unit)


def flip(value, axis, bit):
    count = lax.axis_size(axis)
    return lax.ppermute(value, axis, [(i, i ^ bit) for i in range(count)])


def bits_of(count):
    return [1 << i for i in range(count.bit_length() - 1)]


def cut(value, start, size, axis):
    return lax.slice_in_dim(value, start, start + size, axis=axis)


class Pieces:
    def __init__(self, now, other, order, size, pitch, axis):
        held = [0]
        for bit in order[:-1]:
            held = held + [j ^ bit for j in held]
        self.arrays = (now, other)
        self.where = {}
        for i, j in enumerate(held):
            self.where[j] = (0, i * pitch)
            self.where[j ^ order[-1]] = (1, i * pitch)
        self.size, self.axis = size, axis

    def read(self, refs, j, columns=None):
        side, start = self.where[j]
        if self.axis == 1:
            return refs[side][:, start : start + self.size]
        if columns is None:
            return refs[side][start : start + self.size, :]
        return refs[side][start : start + self.size, columns]


def gather_dp(block, order, axis):
    now = block
    for step, bit in enumerate(order):
        other = flip(now, "dp", bit)
        if step + 1 < len(order):
            now = jnp.concatenate([now, other], axis)
    return now, other


def whole_spec(shape):
    return pl.BlockSpec(shape, lambda i: (0, 0))


def cost(flops, moved):
    return pl.CostEstimate(flops=flops, bytes_accessed=moved, transcendentals=0)


def project_kernel(weight, gelu, x_ref, now_ref, other_ref, row_ref, out_ref, *slope_ref):
    refs = (now_ref, other_ref)
    total = row_ref[...]
    for j in sorted(weight.where):
        x = x_ref[:, j * weight.size : (j + 1) * weight.size]
        total = total + dot(x, weight.read(refs, j), NN)
    if gelu:
        active, slope = gelu_pair(total)
        out_ref[...] = active.astype(half)
        slope_ref[0][...] = slope
    else:
        out_ref[...] = total.astype(half)


def project(x, weight, row, gelu):
    rows, width = x.shape[0], row.shape[0]
    tile = min(width, 256)
    column = lambda i: (0, i)
    shapes = [jax.ShapeDtypeStruct((rows, width), half)]
    if gelu:
        shapes.append(jax.ShapeDtypeStruct((rows, width), single))
    out = call(
        functools.partial(project_kernel, weight, gelu),
        grid=(width // tile,),
        in_specs=[whole_spec(x.shape)]
        + [pl.BlockSpec((a.shape[0], tile), column) for a in weight.arrays]
        + [pl.BlockSpec((1, tile), column)],
        out_specs=[pl.BlockSpec((rows, tile), column) for _ in shapes],
        out_shape=shapes,
        cost_estimate=cost(2 * rows * x.shape[1] * width, 4 * rows * width),
    )(x, *weight.arrays, row[None, :])
    return out if gelu else out[0]


def back_units_kernel(weight, up_ref, now_ref, other_ref, slope_ref, out_ref, sum_ref):
    refs = (now_ref, other_ref)
    total = 0.0
    for j in sorted(weight.where):
        up = up_ref[:, j * weight.size : (j + 1) * weight.size]
        total = total + dot(up, weight.read(refs, j), NT)
    d_pre = total * slope_ref[...]
    out_ref[...] = d_pre.astype(half)
    row = lax.broadcasted_iota(jnp.int32, sum_ref.shape, 0)
    sum_ref[...] = jnp.where(row == 7, jnp.sum(d_pre, axis=0, keepdims=True), 0.0)


def back_units(upstream, weight, slope):
    rows, width = slope.shape
    tile = min(width, 256)
    column = lambda i: (0, i)
    return call(
        functools.partial(back_units_kernel, weight),
        grid=(width // tile,),
        in_specs=[whole_spec(upstream.shape)]
        + [pl.BlockSpec((tile, a.shape[1]), lambda i: (i, 0)) for a in weight.arrays]
        + [pl.BlockSpec((rows, tile), column)],
        out_specs=[pl.BlockSpec((rows, tile), column), pl.BlockSpec((8, tile), column)],
        out_shape=[
            jax.ShapeDtypeStruct((rows, width), half),
            jax.ShapeDtypeStruct((8, width), single),
        ],
        cost_estimate=cost(2 * rows * upstream.shape[1] * width, 6 * rows * width),
    )(upstream, *weight.arrays, slope)


def blend_kernel(weights, columns, dims, *refs):
    out_ref = refs[-1]
    size = weights[0].size
    for j in sorted(weights[0].where):
        total = 0.0
        for c, weight in enumerate(weights):
            left, pair = refs[3 * c], refs[3 * c + 1 : 3 * c + 3]
            if columns is None:
                total = total + dot(left[...], weight.read(pair, j), dims)
                continue
            span = columns[0].stop - columns[0].start
            for g, window in enumerate(columns):
                part = left[:, g * span : (g + 1) * span]
                total = total + dot(part, weight.read(pair, j, window), dims)
        out_ref[:, j * size : (j + 1) * size] = total.astype(half)


def blend(lefts, weights, dims, columns=None):
    rows = lefts[0].shape[0]
    width = weights[0].size * len(weights[0].where)
    tile = min(rows, 256)
    inputs, specs = [], []
    for left, weight in zip(lefts, weights):
        inputs += [left, *weight.arrays]
        specs.append(pl.BlockSpec((tile, left.shape[1]), lambda i: (i, 0)))
        specs += [whole_spec(a.shape) for a in weight.arrays]
    return call(
        functools.partial(blend_kernel, weights, columns, dims),
        grid=(rows // tile,),
        in_specs=specs,
        out_specs=pl.BlockSpec((tile, width), lambda i: (i, 0)),
        out_shape=jax.ShapeDtypeStruct((rows, width), half),
        cost_estimate=cost(4 * rows * width * lefts[0].shape[1], 8 * rows * width),
    )(*inputs)


def back_heads_kernel(weight, columns, up_ref, now_ref, other_ref, out_ref):
    refs = (now_ref, other_ref)
    span = columns[0].stop - columns[0].start
    for g, window in enumerate(columns):
        total = 0.0
        for j in sorted(weight.where):
            up = up_ref[:, j * weight.size : (j + 1) * weight.size]
            total = total + dot(up, weight.read(refs, j, window), NN)
        out_ref[:, g * span : (g + 1) * span] = total.astype(half)


def back_heads(upstream, weight, columns):
    rows = upstream.shape[0]
    width = sum(w.stop - w.start for w in columns)
    return call(
        functools.partial(back_heads_kernel, weight, columns),
        grid=(1,),
        in_specs=[whole_spec(a.shape) for a in (upstream, *weight.arrays)],
        out_specs=whole_spec((rows, width)),
        out_shape=jax.ShapeDtypeStruct((rows, width), half),
        cost_estimate=cost(2 * rows * upstream.shape[1] * width, 8 * rows * width),
    )(upstream, *weight.arrays)


def block_grad_kernel(left_ref, right_ref, out_ref):
    out_ref[...] = dot(left_ref[...], right_ref[...], TN, half)


def block_grad(left, right, wanted, size, rows_cut):
    count = len(wanted)
    first, stride = wanted[0], (wanted[1] - wanted[0] if count > 1 else 1)
    assert wanted == [first + i * stride for i in range(count)]
    rows = left.shape[0]
    chosen = pl.BlockSpec((rows, size), lambda i: (0, first + i * stride))
    if rows_cut:
        specs = [chosen, whole_spec(right.shape)]
        block, index = (size, right.shape[1]), lambda i: (i, 0)
        shape = (count * size, right.shape[1])
    else:
        specs = [whole_spec(left.shape), chosen]
        block, index = (left.shape[1], size), lambda i: (0, i)
        shape = (left.shape[1], count * size)
    return call(
        block_grad_kernel,
        grid=(count,),
        in_specs=specs,
        out_specs=pl.BlockSpec(block, index),
        out_shape=jax.ShapeDtypeStruct(shape, half),
        cost_estimate=cost(2 * rows * shape[0] * shape[1], 4 * shape[0] * shape[1]),
    )(left, right)


def halves(members, bit):
    return [j for j in members if j & bit], [j for j in members if not j & bit]


def scatter_dp(away, stay, order, axis):
    held = list(range(lax.axis_size("dp")))
    for step, bit in enumerate(order):
        other = flip(away, "dp", bit)
        held = halves(held, bit)[1]
        if step + 1 == len(order):
            return (stay.astype(single) + other.astype(single)).astype(half)
        size = stay.shape[axis] // len(held)

        def pick(value, wanted):
            parts = [cut(value, held.index(j) * size, size, axis) for j in wanted]
            return parts[0] if len(parts) == 1 else jnp.concatenate(parts, axis)

        def added(wanted):
            total = pick(stay, wanted).astype(single) + pick(other, wanted).astype(single)
            return total.astype(half)

        away, stay = (added(part) for part in halves(held, order[step + 1]))


def gather_z(shard, axis):
    bits = bits_of(lax.axis_size("z"))
    now = shard
    for bit in bits[:-1]:
        now = jnp.concatenate([now, flip(now, "z", bit)], axis)
    return now, flip(now, "z", bits[-1])


def scatter_z(colors, axis):
    bits = bits_of(lax.axis_size("z"))
    held = list(range(1 << len(bits)))
    size = colors[0].shape[axis] * 2 // len(held)
    slots = [cut(color, i * size, size, axis) for color in colors for i in range(len(held) // 2)]
    for bit in bits:
        leave, stay = halves(held, bit)
        parts = [[slots[held.index(r)] for r in group] for group in (leave, stay)]
        away, keep = (p[0] if len(p) == 1 else jnp.concatenate(p, axis) for p in parts)
        other = flip(away, "z", bit)
        if bit == bits[-1]:
            return keep, other
        total = (keep.astype(single) + other.astype(single)).astype(half)
        held = stay
        slots = [cut(total, i * size, size, axis) for i in range(len(held))]


def added(pair):
    return pair[0].astype(single) + pair[1].astype(single)


def first_update_kernel(
    keep_ref, other_ref, qkv_ref, qkv_m_ref, proj_ref, proj_m_ref,
    sum_ref, proj_sum_ref, new_ref, proj_new_ref, state_ref, proj_state_ref, small_ref,
):
    size, width = qkv_ref.shape[1:]
    grad = keep_ref[...].astype(single) + other_ref[...].astype(single)
    small_ref[...] = grad[size:]

    def step(weight, first, second, total):
        first = beta_one * first + (1.0 - beta_one) * total
        second = beta_two * second + (1.0 - beta_two) * total * total
        scale_one = 1.0 - beta_one**STEP
        scale_two = 1.0 - beta_two**STEP
        update = first / scale_one / (jnp.sqrt(second / scale_two) + adam_eps)
        return weight - learn_rate * (update + decay_rate * weight), first, second

    for j in range(3):
        total = grad[:size, j * width : (j + 1) * width]
        sum_ref[j] = total
        new, first, second = step(qkv_ref[j], qkv_m_ref[0, j], qkv_m_ref[1, j], total)
        new_ref[j] = new
        state_ref[0, j] = first
        state_ref[1, j] = second
    total = grad[:size, 3 * width :].T
    proj_sum_ref[...] = total
    new, first, second = step(proj_ref[...], proj_m_ref[0], proj_m_ref[1], total)
    proj_new_ref[...] = new
    proj_state_ref[0] = first
    proj_state_ref[1] = second


def first_update(pair, qkv, qkv_m, proj, proj_m):
    extra = pair[0].shape[0] - qkv.shape[1]
    shapes = [a.shape for a in (qkv, proj, qkv, proj, qkv_m, proj_m)]
    shapes.append((extra, pair[0].shape[1]))
    operands = (*pair, qkv, qkv_m, proj, proj_m)

    def full(shape):
        return pl.BlockSpec(shape, lambda i: (0,) * len(shape))

    return call(
        first_update_kernel,
        grid=(1,),
        in_specs=[full(a.shape) for a in operands],
        out_specs=[full(shape) for shape in shapes],
        out_shape=[jax.ShapeDtypeStruct(shape, single) for shape in shapes],
        cost_estimate=cost(20 * qkv.size, 40 * qkv.size),
    )(*operands)


def sum_members(term):
    now = term
    bits = bits_of(lax.axis_size("g"))
    for bit in bits:
        other = flip(now, "g", bit)
        if bit != bits[-1]:
            now = (now.astype(single) + other.astype(single)).astype(half)
    return now, other


def gather_members(rows):
    me = lax.axis_index("g")
    for bit in bits_of(lax.axis_size("g")):
        other = flip(rows, "g", bit)
        rows = jnp.where(
            (me & bit) != 0,
            jnp.concatenate([other, rows], 0),
            jnp.concatenate([rows, other], 0),
        )
    return rows


def scatter_members(term):
    me = lax.axis_index("g")
    now = term.astype(half)
    for bit in reversed(bits_of(lax.axis_size("g"))):
        size = now.shape[0] // 2
        side = ((me & bit) != 0).astype(jnp.int32)
        send = lax.dynamic_slice_in_dim(now, (1 - side) * size, size, 0)
        keep = lax.dynamic_slice_in_dim(now, side * size, size, 0)
        total = keep.astype(single) + flip(send, "g", bit).astype(single)
        now = total.astype(half)
    return total


def reorder(matrix, count, member):
    size = matrix.shape[-1] // count
    return jnp.concatenate(
        [
            lax.dynamic_slice_in_dim(matrix, (member ^ j) * size, size, matrix.ndim - 1)
            for j in range(count)
        ],
        -1,
    )


def layer_step(
    block_in,
    cotangent,
    lengths,
    qkv_weight,
    proj_weight,
    expand_weight,
    reduce_weight,
    split_bias,
    vector_params,
    qkv_moments,
    proj_moments,
    expand_moments,
    reduce_moments,
    bias_moments,
    vector_moments,
):
    n_dp, n_z = lax.axis_size("dp"), lax.axis_size("z")
    dp, z, member = lax.axis_index("dp"), lax.axis_index("z"), lax.axis_index("g")
    share = block_in.shape[0]
    model = block_in.shape[1]
    width = qkv_weight.shape[2]
    part = model // n_dp
    heads = split_bias.shape[0]
    bias_part = split_bias.shape[1]
    pair = n_z // 2
    ganged = 1 if width % LANES == 0 else pair
    gang = ganged * width
    per = gang // LANES
    up = bits_of(n_dp)
    down = up[::-1]
    order_q, order_e, order_r = (up, up), (down, up), (down, up)
    extra = -(-max(6 + heads, 8) // 16) * 16

    def wide(rows, count):
        return jnp.pad(rows, ((0, 0), (0, count - rows.shape[1])))

    small = jnp.concatenate(
        [
            wide(vector_params.astype(half), 4 * width),
            wide(split_bias.astype(half), 4 * width),
            jnp.zeros((extra - 6 - heads, 4 * width), half),
        ],
        0,
    )
    own_q = jnp.concatenate(
        [qkv_weight[j].astype(half) for j in range(3)] + [proj_weight.astype(half).T], 1
    )
    own_q = jnp.concatenate([own_q, small], 0)
    own_e = expand_weight.astype(half)
    own_r = reduce_weight.astype(half)

    weight_q, weight_e, weight_r, small_q = [], [], [], []

    def ganged_columns(matrix):
        if ganged == 1:
            return matrix
        cut_up = matrix.reshape(matrix.shape[0], -1, ganged, 4, width)
        return cut_up.transpose(0, 1, 3, 2, 4).reshape(matrix.shape)

    for c, block in enumerate(gather_z(own_q, 1)):
        arrays = gather_dp(block, order_q[c], 0)
        held = Pieces(*arrays, order_q[c], extra, part + extra, 0)
        small_q.append(
            [
                cut(arrays[held.where[j][0]], held.where[j][1] + part, extra, 0)
                for j in range(n_dp)
            ]
        )
        arrays = [ganged_columns(a) for a in arrays]
        weight_q.append(Pieces(*arrays, order_q[c], part, part + extra, 0))
    for c, block in enumerate(gather_z(own_e, 1)):
        arrays = gather_dp(block, order_e[c], 0)
        weight_e.append(Pieces(*arrays, order_e[c], part, part, 0))
    for c, block in enumerate(gather_z(own_r, 0)):
        arrays = gather_dp(block, order_r[c], 1)
        weight_r.append(Pieces(*arrays, order_r[c], part, part, 1))

    vectors = jnp.concatenate([small_q[0][j][:6, :part] for j in range(n_dp)], 1)
    vectors = jnp.pad(vectors.astype(single), ((0, 2), (0, 0)))
    mine_at = jnp.arange(n_dp, dtype=jnp.int32)
    picked = ((mine_at[:, None] ^ dp) == mine_at[None, :]).astype(half)

    def biases_of(small_rows):
        rel = jnp.stack([p[6 : 6 + heads] for p in small_rows])
        rel = rel.reshape(n_dp, heads, pair, 4 * width)[..., :bias_part]
        rows = dot(picked, rel.reshape(n_dp, -1), NN).reshape(n_dp, heads, pair, bias_part)
        return rows.transpose(2, 1, 0, 3).reshape(pair, heads, -1)

    length = lax.dynamic_index_in_dim(lengths, z, 0, keepdims=False)
    live = jnp.arange(L, dtype=jnp.int32) < length
    mask = jnp.where(live, 0.0, -jnp.inf).astype(single)[None, :]
    live_rows = jnp.broadcast_to(live[:, None].astype(single), (L, LANES))

    x_full = gather_members(reorder(block_in, n_dp, dp))
    up_full = gather_members(reorder(cotangent, n_dp, dp))

    projected, heads_out, lse, bias_rows = [], [], [], []
    groups = pair // ganged
    out_columns = [slice((4 * i + 3) * gang, (4 * i + 4) * gang) for i in range(groups)]
    for c in range(2):
        if c:
            small_q[c], projected[0] = lax.optimization_barrier((small_q[c], projected[0]))
        bias_rows.append(biases_of(small_q[c]))
        rows = bias_rows[c].reshape(groups, ganged, heads, -1)
        q_bias = rows[..., :HD].reshape(groups, gang)
        v_bias = rows[..., HD : 2 * HD].reshape(groups, gang)
        nothing = jnp.zeros_like(q_bias)
        row = jnp.concatenate([q_bias, nothing, v_bias, nothing], 1).reshape(-1)
        projected.append(project(x_full, weight_q[c], row, False))
        out, log_total = attend(projected[c], mask, per)
        heads_out.append(out)
        lse.append(log_total)
    attn_term = blend(heads_out, weight_q, NT, out_columns)
    mine, other = sum_members(attn_term)
    hidden_f, hidden_b, normed_one, inv_one = by_rows(
        first_norm_kernel,
        (x_full, mine, other, vectors),
        ((model, single), (model, half), (model, single), (LANES, single)),
        0,
    )
    active_b, slopes = [], []
    for c in range(2):
        row = bias_rows[c][..., 2 * HD :].reshape(-1)
        active, slope = project(hidden_b, weight_e[c], row, True)
        active_b.append(active)
        slopes.append(slope)
    ffn_term = blend(active_b, weight_r, NN)
    mine, other = sum_members(ffn_term)
    out_b, d_two, d_two_b, sums_two = by_rows(
        second_norm_kernel,
        (hidden_f, mine, other, up_full, live_rows, vectors),
        ((model, half), (model, single), (model, half)),
        model,
    )

    members = list(range(n_dp))
    firsts = (down[0], up[0])
    back = (down, up)
    got_r, got_e, got_q = [], [], []
    sent_r = []
    for c in range(2):
        sent_r.append(block_grad(active_b[c], d_two_b, halves(members, firsts[c])[0], part, False))
    for c in range(2):
        kept = block_grad(active_b[c], d_two_b, halves(members, firsts[c])[1], part, False)
        got_r.append(scatter_dp(sent_r[c], kept, back[c], 1))
    unit_sums, d_pre_b = [], []
    for c in range(2):
        d_pre, sums = back_units(d_two_b, weight_r[c], slopes[c])
        unit_sums.append(sums)
        d_pre_b.append(d_pre)
    hidden_term = blend(d_pre_b, weight_e, NT)
    for c in range(2):
        leave, kept = halves(members, firsts[c])
        leave = block_grad(hidden_b, d_pre_b[c], leave, part, True)
        kept = block_grad(hidden_b, d_pre_b[c], kept, part, True)
        got_e.append(scatter_dp(leave, kept, back[c], 0))
    mine, other = sum_members(hidden_term)
    d_one, d_one_b, sums_one = by_rows(
        first_back_kernel,
        (d_two, mine, other, normed_one, inv_one, vectors),
        ((model, single), (model, half)),
        model,
    )
    vec = (sums_one + sums_two).reshape(8, n_dp, 1, part)
    vec = jnp.pad(vec, ((0, 0), (0, 0), (0, 0), (0, 4 * width - part)))
    vec = jnp.broadcast_to(vec, (8, n_dp, pair, 4 * width)).reshape(8, -1)
    vec = ganged_columns(vec)
    stacks = []
    for c in range(2):
        d_heads = back_heads(d_one_b, weight_q[c], out_columns)
        d_stack, sums = attend_back(projected[c], d_heads, lse[c], mask, per)
        stacks.append(d_stack)
        unit = ganged_columns(unit_sums[c])
        leave, kept = halves(members, firsts[c])
        operands = (x_full, d_stack, d_one_b, heads_out[c], vec, sums, unit)
        leave = first_grad(*operands, leave, part, per, extra)
        kept = first_grad(*operands, kept, part, per, extra)
        got_q.append(scatter_dp(leave, kept, back[c], 0))
    if ganged > 1:
        got_q = [
            g.reshape(part + extra, -1, 4, ganged, width)
            .transpose(0, 1, 3, 2, 4)
            .reshape(part + extra, -1)
            for g in got_q
        ]

    reduce_sum = added(scatter_z(got_r, 0))
    expand_sum = added(scatter_z(got_e, 1))
    qkv_sum, proj_sum, qkv_new, proj_new, qkv_state, proj_state, packed = first_update(
        scatter_z(got_q, 1), qkv_weight, qkv_moments, proj_weight, proj_moments
    )
    vector_sum = packed[:6, :part]
    bias_all = jnp.concatenate(
        [
            packed[6, :width].reshape(heads, HD),
            packed[6, 2 * width : 3 * width].reshape(heads, HD),
            packed[7].reshape(heads, -1),
        ],
        1,
    )
    bias_sum = lax.dynamic_slice_in_dim(bias_all, dp * bias_part, bias_part, 1)

    out_b, stacks = lax.optimization_barrier((out_b, stacks))
    input_term = blend(stacks, weight_q, NT)
    first_row = member * share
    block_out = reorder(lax.dynamic_slice_in_dim(out_b, first_row, share, 0), n_dp, dp)
    own_one = lax.dynamic_slice_in_dim(d_one, first_row, share, 0)
    input_grad = reorder((own_one + scatter_members(input_term)).astype(half), n_dp, dp)

    expand_new, expand_state = adamw_step(expand_weight, expand_moments, expand_sum, decay_rate)
    reduce_new, reduce_state = adamw_step(reduce_weight, reduce_moments, reduce_sum, decay_rate)
    bias_new, bias_state = adamw_step(split_bias, bias_moments, bias_sum, 0.0)
    vector_new, vector_state = adamw_step(vector_params, vector_moments, vector_sum, 0.0)
    return (
        block_out,
        input_grad,
        qkv_sum,
        proj_sum,
        expand_sum,
        reduce_sum,
        bias_sum,
        vector_sum,
        qkv_new,
        proj_new,
        expand_new,
        reduce_new,
        bias_new,
        vector_new,
        qkv_state,
        proj_state,
        expand_state,
        reduce_state,
        bias_state,
        vector_state,
    )


def solution(mesh):
    n_dp, n_tensor = mesh.devices.shape

    def step(*args):
        share = args[0].shape[0] // (n_dp * n_tensor)
        members = L // share
        inner = Mesh(
            mesh.devices.reshape(n_dp, n_tensor // members, members), ("dp", "z", "g")
        )
        tensor = ("z", "g")
        rows = P(("dp", "z", "g"), None)
        weights = (
            P(None, "dp", tensor),
            P(tensor, "dp"),
            P("dp", tensor),
            P(tensor, "dp"),
            P(tensor, "dp"),
            P(None, "dp"),
        )
        states = (
            P(None, None, "dp", tensor),
            P(None, tensor, "dp"),
            P(None, "dp", tensor),
            P(None, tensor, "dp"),
            P(None, tensor, "dp"),
            P(None, None, "dp"),
        )
        placed = jax.shard_map(
            layer_step,
            mesh=inner,
            in_specs=(rows, rows, P("dp")) + weights + states,
            out_specs=(rows, rows) + weights + weights + states,
            check_vma=False,
        )
        return placed(*args)

    return step
```

profile of v0, /device:TPU:0, one launch (start us, length us, event | category | flops | bytes accessed | tf_op | source)
XLA Modules:
  0.0 376.2 jit_solution(1301632294660528607)
XLA Ops:
  3.7 3.1 collective-permute-start.1
  7.0 2.1 collective-permute-start.11
  9.0 5.3 %collective-permute-done.1 = bf16[272,512]{1,0:T(8,128)(2,1)S(1)} collective-permute-done((bf16[272,512]{1,0:T(8,128)(2,1)S(1)}, bf16[272,512]{1,0:T(8,128)(2,1)S(1)}, u32[]{:S(2)}, u32[]{:S(2)}) %collective-permute-start.1) | collective-permute-done | bytes 278560 | tf_op jit(solution)/shard_map/ppermute | solution.py:302
  15.2 1.9 collective-permute-start.2
  17.1 2.1 constant_dynamic-slice_fusion.11
  21.4 2.7 collective-permute-start.4
  33.2 28.1 %collective-permute-done.4 = bf16[272,1024]{1,0:T(8,128)(2,1)} collective-permute-done((bf16[272,1024]{1,0:T(8,128)(2,1)}, bf16[272,1024]{1,0:T(8,128)(2,1)}, u32[]{:S(2)}, u32[]{:S(2)}) %collective-permute-start.4) | collective-permute-done | bytes 557088 | tf_op jit(solution)/shard_map/ppermute | solution.py:302
  63.1 9.0 %collective-permute-done.14 = bf16[256,1024]{1,0:T(8,128)(2,1)} collective-permute-done((bf16[256,1024]{1,0:T(8,128)(2,1)}, bf16[256,1024]{1,0:T(8,128)(2,1)}, u32[]{:S(2)}, u32[]{:S(2)}) %collective-permute-start.14) | collective-permute-done | bytes 524320 | tf_op jit(solution)/shard_map/ppermute | solution.py:302
  72.1 1.9 constant_dynamic-update-slice_fusion.3
  74.5 2.1 pad_maximum_fusion.1.now_ref.refs_1_
  78.1 2.2 pad_maximum_fusion.2.refs_1_.now_ref
  81.8 2.0 constant_dynamic-update-slice_fusion.1
  83.8 14.3 %collective-permute-done.17 = bf16[1024,256]{1,0:T(8,128)(2,1)} collective-permute-done((bf16[1024,256]{1,0:T(8,128)(2,1)}, bf16[1024,256]{1,0:T(8,128)(2,1)}, u32[]{:S(2)}, u32[]{:S(2)}) %collective-permute-start.17) | collective-permute-done | bytes 524320 | tf_op jit(solution)/shard_map/ppermute | solution.py:302
  100.0 1.9 constant_dynamic-update-slice_fusion.now_ref.refs_4_
  107.1 3.7 shard_map.302.q_ref.k_ref.v_ref
  110.7 3.0 shard_map.303
  114.6 15.1 %collective-permute-done.6.other_ref.refs_5_ = bf16[544,1024]{1,0:T(8,128)(2,1)} collective-permute-done((bf16[544,1024]{1,0:T(8,128)(2,1)}, bf16[544,1024]{1,0:T(8,128)(2,1)}, u32[]{:S(2)}, u32[]{:S(2)}) %collective-permute-start.6) | collective-permute-done | bytes 1114144 | tf_op jit(solution)/shard_map/ppermute | solution.py:302
  131.3 3.6 shard_map.304.q_ref.k_ref.v_ref
  134.9 3.0 shard_map.305
  137.9 3.7 shard_map.306.mine_ref
  141.7 2.2 constant_dynamic-update-slice_fusion.5
  143.9 1.9 constant_dynamic-update-slice_fusion.4.refs_4_.now_ref
  150.2 2.9 shard_map.307
  155.1 4.4 %shard_map.309 = (bf16[512,1024]{1,0:T(8,128)(2,1)S(1)}, f32[512,1024]{1,0:T(8,128)S(1)}) custom-call(bf16[512,1024]{1,0:T(8,128)(2,1)S(1)} %get-tuple-element.69.x_ref.left_ref, bf16[512,1024]{1,0:T(8,128)(2,1)} %constant_dynamic-update-slice_fusion.2.now_ref.refs_4_, bf16[512,1024]{1,0:T(8,128)(2,1)} %collective-permute-done.16.other_ref.refs_5_, ...), custom_call_target="tpu_custom_call" | custom-call | flops 1073741824 | bytes 2097152 | tf_op jit(solution)/shard_map/pallas_call | solution.py:372
  159.6 4.4 %shard_map.308 = (bf16[512,1024]{1,0:T(8,128)(2,1)S(1)}, f32[512,1024]{1,0:T(8,128)S(1)}) custom-call(bf16[512,1024]{1,0:T(8,128)(2,1)S(1)} %get-tuple-element.69.x_ref.left_ref, bf16[512,1024]{1,0:T(8,128)(2,1)} %pad_maximum_fusion.1.now_ref.refs_1_, bf16[512,1024]{1,0:T(8,128)(2,1)} %collective-permute-done.10.other_ref.refs_2_, ...), custom_call_target="tpu_custom_call" | custom-call | flops 1073741824 | bytes 2097152 | tf_op jit(solution)/shard_map/pallas_call | solution.py:372
  164.0 7.9 %collective-permute-done.19.refs_5_.other_ref = bf16[1024,512]{1,0:T(8,128)(2,1)} collective-permute-done((bf16[1024,512]{1,0:T(8,128)(2,1)}, bf16[1024,512]{1,0:T(8,128)(2,1)}, u32[]{:S(2)}, u32[]{:S(2)}) %collective-permute-start.19) | collective-permute-done | bytes 1048608 | tf_op jit(solution)/shard_map/ppermute | solution.py:302
  171.9 4.8 %shard_map.310.mine_ref = bf16[512,1024]{1,0:T(8,128)(2,1)S(1)} custom-call(bf16[512,1024]{1,0:T(8,128)(2,1)S(1)} %get-tuple-element.70.refs_0_.left_ref, bf16[1024,512]{1,0:T(8,128)(2,1)} %pad_maximum_fusion.2.refs_1_.now_ref, bf16[1024,512]{1,0:T(8,128)(2,1)} %collective-permute-done.13.refs_2_.other_ref, ...), custom_call_target="tpu_custom_call" | custom-call | flops 2147483648 | bytes 4194304 | tf_op jit(solution)/shard_map/pallas_call | solution.py:442
  178.1 2.1 collective-permute-done.21
  180.8 2.4 shard_map.311
  184.5 4.0 %shard_map.313 = (bf16[512,1024]{1,0:T(8,128)(2,1)S(1)}, f32[8,1024]{1,0:T(8,128)S(1)}) custom-call(bf16[512,1024]{1,0:T(8,128)(2,1)S(1)} %get-tuple-element.75.up_ref.right_ref, bf16[1024,512]{1,0:T(8,128)(2,1)} %constant_dynamic-update-slice_fusion.4.refs_4_.now_ref, bf16[1024,512]{1,0:T(8,128)(2,1)} %collective-permute-done.19.refs_5_.other_ref, ...), custom_call_target="tpu_custom_call" | custom-call | flops 1073741824 | bytes 3145728 | tf_op jit(solution)/shard_map/pallas_call | solution.py:401
  188.6 4.1 %shard_map.312 = (bf16[512,1024]{1,0:T(8,128)(2,1)S(1)}, f32[8,1024]{1,0:T(8,128)S(1)}) custom-call(bf16[512,1024]{1,0:T(8,128)(2,1)S(1)} %get-tuple-element.75.up_ref.right_ref, bf16[1024,512]{1,0:T(8,128)(2,1)} %pad_maximum_fusion.2.refs_1_.now_ref, bf16[1024,512]{1,0:T(8,128)(2,1)} %collective-permute-done.13.refs_2_.other_ref, ...), custom_call_target="tpu_custom_call" | custom-call | flops 1073741824 | bytes 3145728 | tf_op jit(solution)/shard_map/pallas_call | solution.py:401
  193.3 5.9 %shard_map.314.mine_ref = bf16[512,1024]{1,0:T(8,128)(2,1)} custom-call(bf16[512,1024]{1,0:T(8,128)(2,1)S(1)} %get-tuple-element.77.refs_0_.right_ref, bf16[512,1024]{1,0:T(8,128)(2,1)} %pad_maximum_fusion.1.now_ref.refs_1_, bf16[512,1024]{1,0:T(8,128)(2,1)} %collective-permute-done.10.other_ref.refs_2_, ...), custom_call_target="tpu_custom_call" | custom-call | flops 2147483648 | bytes 4194304 | tf_op jit(solution)/shard_map/pallas_call | solution.py:442
  215.4 3.4 shard_map.315
  218.9 2.1 shard_map.316.up_ref
  221.0 4.7 %shard_map.317 = (bf16[512,1024]{1,0:T(8,128)(2,1)S(1)}, f32[8,1024]{1,0:T(8,128)S(1)}) custom-call(bf16[512,1024]{1,0:T(8,128)(2,1)S(1)} %copy-done.3, bf16[512,1024]{1,0:T(8,128)(2,1)S(1)} %copy-done.3, bf16[512,1024]{1,0:T(8,128)(2,1)S(1)} %copy-done.3, bf16[512,256]{1,0:T(8,128)(2,1)S(1)} %shard_map.316.up_ref, f32[512,256]{1,0:T(8,128)S(1)} %copy-done.36, ...), custom_call_target="tpu_custom_call" | custom-call | flops 1342177280 | bytes 3145728 | tf_op jit(solution)/shard_map/pallas_call | solution.py:142
  228.7 2.3 shard_map.318.up_ref
  231.0 4.7 %shard_map.319 = (bf16[512,1024]{1,0:T(8,128)(2,1)S(1)}, f32[8,1024]{1,0:T(8,128)S(1)}) custom-call(bf16[512,1024]{1,0:T(8,128)(2,1)S(1)} %copy-done.5, bf16[512,1024]{1,0:T(8,128)(2,1)S(1)} %copy-done.5, bf16[512,1024]{1,0:T(8,128)(2,1)S(1)} %copy-done.5, bf16[512,256]{1,0:T(8,128)(2,1)S(1)} %shard_map.318.up_ref, f32[512,256]{1,0:T(8,128)S(1)} %copy-done.38, ...), custom_call_target="tpu_custom_call" | custom-call | flops 1342177280 | bytes 3145728 | tf_op jit(solution)/shard_map/pallas_call | solution.py:142
  237.1 4.6 %shard_map.320 = bf16[512,1024]{1,0:T(8,128)(2,1)S(1)} custom-call(bf16[512,1024]{1,0:T(8,128)(2,1)S(1)} %get-tuple-element.89.refs_0_.stack_ref, bf16[544,1024]{1,0:T(8,128)(2,1)S(1)} %pad_maximum_fusion.now_ref.refs_1_, bf16[544,1024]{1,0:T(8,128)(2,1)} %collective-permute-done.3.other_ref.refs_2_, ...), custom_call_target="tpu_custom_call" | custom-call | flops 2147483648 | bytes 4194304 | tf_op jit(solution)/shard_map/pallas_call | solution.py:442
  248.3 2.7 collective-permute-done.30
  254.6 34.3 %collective-permute-done.37 = bf16[1024,256]{1,0:T(8,128)(2,1)S(1)} collective-permute-done((bf16[1024,256]{1,0:T(8,128)(2,1)S(1)}, bf16[1024,256]{1,0:T(8,128)(2,1)S(1)}, u32[]{:S(2)}, u32[]{:S(2)}) %collective-permute-start.37) | collective-permute-done | bytes 524320 | tf_op jit(solution)/shard_map/ppermute | solution.py:302
  290.2 9.2 %collective-permute-done.31 = bf16[256,1024]{1,0:T(8,128)(2,1)S(1)} collective-permute-done((bf16[256,1024]{1,0:T(8,128)(2,1)S(1)}, bf16[256,1024]{1,0:T(8,128)(2,1)S(1)}, u32[]{:S(2)}, u32[]{:S(2)}) %collective-permute-start.31) | collective-permute-done | bytes 524320 | tf_op jit(solution)/shard_map/ppermute | solution.py:302
  299.3 2.4 collective-permute-start.40
  305.3 9.3 %collective-permute-done.40 = bf16[1024,256]{1,0:T(8,128)(2,1)S(1)} collective-permute-done((bf16[1024,256]{1,0:T(8,128)(2,1)S(1)}, bf16[1024,256]{1,0:T(8,128)(2,1)S(1)}, u32[]{:S(2)}, u32[]{:S(2)}) %collective-permute-start.40) | collective-permute-done | bytes 524320 | tf_op jit(solution)/shard_map/ppermute | solution.py:302
  315.3 14.6 %collective-permute-done.34 = bf16[256,1024]{1,0:T(8,128)(2,1)S(1)} collective-permute-done((bf16[256,1024]{1,0:T(8,128)(2,1)S(1)}, bf16[256,1024]{1,0:T(8,128)(2,1)S(1)}, u32[]{:S(2)}, u32[]{:S(2)}) %collective-permute-start.34) | collective-permute-done | bytes 524320 | tf_op jit(solution)/shard_map/ppermute | solution.py:302
  333.8 8.8 %collective-permute-done.35 = bf16[256,512]{1,0:T(8,128)(2,1)S(1)} collective-permute-done((bf16[256,512]{1,0:T(8,128)(2,1)S(1)}, bf16[256,512]{1,0:T(8,128)(2,1)S(1)}, u32[]{:S(2)}, u32[]{:S(2)}) %collective-permute-start.35) | collective-permute-done | bytes 262176 | tf_op jit(solution)/shard_map/ppermute | solution.py:302
  348.9 9.2 %collective-permute-done.28 = bf16[272,1024]{1,0:T(8,128)(2,1)S(1)} collective-permute-done((bf16[272,1024]{1,0:T(8,128)(2,1)S(1)}, bf16[272,1024]{1,0:T(8,128)(2,1)S(1)}, u32[]{:S(2)}, u32[]{:S(2)}) %collective-permute-start.28) | collective-permute-done | bytes 557088 | tf_op jit(solution)/shard_map/ppermute | solution.py:302
  360.8 10.6 %collective-permute-done.29.other_ref = bf16[272,512]{1,0:T(8,128)(2,1)S(1)} collective-permute-done((bf16[272,512]{1,0:T(8,128)(2,1)S(1)}, bf16[272,512]{1,0:T(8,128)(2,1)S(1)}, u32[]{:S(2)}, u32[]{:S(2)}) %collective-permute-start.29) | collective-permute-done | bytes 278560 | tf_op jit(solution)/shard_map/ppermute | solution.py:302
  371.5 1.9 shard_map.325
  (350 shorter events, 91.9 us)
Async XLA Ops:
  3.7 10.6 %collective-permute-start.1 = (bf16[272,512]{1,0:T(8,128)(2,1)S(1)}, bf16[272,512]{1,0:T(8,128)(2,1)S(1)}, u32[]{:S(2)}, u32[]{:S(2)}) collective-permute-start(bf16[272,512]{1,0:T(8,128)(2,1)S(1)} %pad_maximum_fusion.13), channel_id=1, source_target_pairs={{0,2},{2,0},{4,6},{6,4},{1,3},{3,1},{5,7},{7,5},{8,10},{10,8},{12,... | collective-permute-start | bytes 835592 | tf_op jit(solution)/shard_map/ppermute | solution.py:302
  6.8 17.2 %collective-permute-start.8 = (bf16[256,512]{1,0:T(8,128)(2,1)S(1)}, bf16[256,512]{1,0:T(8,128)(2,1)S(1)}, u32[]{:S(2)}, u32[]{:S(2)}) collective-permute-start(bf16[256,512]{1,0:T(8,128)(2,1)S(1)} %convert_element_type.264), channel_id=1, source_target_pairs={{0,2},{2,0},{4,6},{6,4},{1,3},{3,1},{5,7},{7,5},{8,10},{10,8},{12,... | collective-permute-start | bytes 786440 | tf_op jit(solution)/shard_map/ppermute | solution.py:302
  7.0 18.3 %collective-permute-start.11 = (bf16[512,256]{1,0:T(8,128)(2,1)S(1)}, bf16[512,256]{1,0:T(8,128)(2,1)S(1)}, u32[]{:S(2)}, u32[]{:S(2)}) collective-permute-start(bf16[512,256]{1,0:T(8,128)(2,1)S(1)} %convert_element_type.265), channel_id=1, source_target_pairs={{0,2},{2,0},{4,6},{6,4},{1,3},{3,1},{5,7},{7,5},{8,10},{10,8},{12,... | collective-permute-start | bytes 786440 | tf_op jit(solution)/shard_map/ppermute | solution.py:302
  15.2 13.2 %collective-permute-start.2 = (bf16[272,1024]{1,0:T(8,128)(2,1)}, bf16[272,1024]{1,0:T(8,128)(2,1)S(1)}, u32[]{:S(2)}, u32[]{:S(2)}) collective-permute-start(bf16[272,1024]{1,0:T(8,128)(2,1)} %pad_maximum_fusion.3), channel_id=1, source_target_pairs={{0,8},{8,0},{16,24},{24,16},{1,9},{9,1},{17,25},{25,17},{2,10},{10... | collective-permute-start | bytes 1671176 | tf_op jit(solution)/shard_map/ppermute | solution.py:302
  20.1 11.7 %collective-permute-start = (bf16[256,1024]{1,0:T(8,128)(2,1)}, bf16[256,1024]{1,0:T(8,128)(2,1)}, u32[]{:S(2)}, u32[]{:S(2)}) collective-permute-start(bf16[256,1024]{1,0:T(8,128)(2,1)} %pad_maximum_fusion.5), channel_id=1, source_target_pairs={{0,1},{1,0},{2,3},{3,2},{4,5},{5,4},{6,7},{7,6},{8,9},{9,8},{10,11... | collective-permute-start | bytes 1572872 | tf_op jit(solution)/shard_map/ppermute | solution.py:302
  21.4 40.0 %collective-permute-start.4 = (bf16[272,1024]{1,0:T(8,128)(2,1)}, bf16[272,1024]{1,0:T(8,128)(2,1)}, u32[]{:S(2)}, u32[]{:S(2)}) collective-permute-start(bf16[272,1024]{1,0:T(8,128)(2,1)} %pad_maximum_fusion.3), channel_id=1, source_target_pairs={{0,4},{2,6},{4,0},{6,2},{1,5},{3,7},{5,1},{7,3},{8,12},{10,14},{12... | collective-permute-start | bytes 1671176 | tf_op jit(solution)/shard_map/ppermute | solution.py:302
  24.9 47.2 %collective-permute-start.14 = (bf16[256,1024]{1,0:T(8,128)(2,1)}, bf16[256,1024]{1,0:T(8,128)(2,1)}, u32[]{:S(2)}, u32[]{:S(2)}) collective-permute-start(bf16[256,1024]{1,0:T(8,128)(2,1)} %pad_maximum_fusion.6), channel_id=1, source_target_pairs={{0,4},{2,6},{4,0},{6,2},{1,5},{3,7},{5,1},{7,3},{8,12},{10,14},{12... | collective-permute-start | bytes 1572872 | tf_op jit(solution)/shard_map/ppermute | solution.py:302
  25.2 48.7 %collective-permute-start.9 = (bf16[256,1024]{1,0:T(8,128)(2,1)}, bf16[256,1024]{1,0:T(8,128)(2,1)}, u32[]{:S(2)}, u32[]{:S(2)}) collective-permute-start(bf16[256,1024]{1,0:T(8,128)(2,1)} %pad_maximum_fusion.6), channel_id=1, source_target_pairs={{0,16},{8,24},{16,0},{24,8},{1,17},{9,25},{17,1},{25,9},{2,18},{10... | collective-permute-start | bytes 1572872 | tf_op jit(solution)/shard_map/ppermute | solution.py:302
  29.2 47.5 %collective-permute-start.12 = (bf16[1024,256]{1,0:T(8,128)(2,1)}, bf16[1024,256]{1,0:T(8,128)(2,1)}, u32[]{:S(2)}, u32[]{:S(2)}) collective-permute-start(bf16[1024,256]{1,0:T(8,128)(2,1)} %pad_maximum_fusion.7), channel_id=1, source_target_pairs={{0,16},{8,24},{16,0},{24,8},{1,17},{9,25},{17,1},{25,9},{2,18},{10... | collective-permute-start | bytes 1572872 | tf_op jit(solution)/shard_map/ppermute | solution.py:302
  31.8 73.3 %collective-permute-start.3 = (bf16[544,1024]{1,0:T(8,128)(2,1)S(1)}, bf16[544,1024]{1,0:T(8,128)(2,1)}, u32[]{:S(2)}, u32[]{:S(2)}) collective-permute-start(bf16[544,1024]{1,0:T(8,128)(2,1)S(1)} %pad_maximum_fusion.now_ref.refs_1_), channel_id=1, source_target_pairs={{0,16},{8,24},{16,0},{24,8},{1,17},{9,25},{17,1},{25,9},{2,18},{10... | collective-permute-start | bytes 3342344 | tf_op jit(solution)/shard_map/ppermute | solution.py:302
  33.2 41.3 %copy-start.56 = (bf16[256,512]{1,0:T(8,128)(2,1)S(1)}, bf16[256,512]{1,0:T(8,128)(2,1)}, u32[]{:S(2)}) copy-start(bf16[256,512]{1,0:T(8,128)(2,1)} %copy-done.55) | copy-start | bytes 786436
  61.3 37.5 %collective-permute-start.5 = (bf16[272,1024]{1,0:T(8,128)(2,1)}, bf16[272,1024]{1,0:T(8,128)(2,1)}, u32[]{:S(2)}, u32[]{:S(2)}) collective-permute-start(bf16[272,1024]{1,0:T(8,128)(2,1)} %collective-permute-done.4), channel_id=1, source_target_pairs={{0,8},{8,0},{16,24},{24,16},{1,9},{9,1},{17,25},{25,17},{2,10},{10... | collective-permute-start | bytes 1671176 | tf_op jit(solution)/shard_map/ppermute | solution.py:302
  72.1 25.9 %collective-permute-start.17 = (bf16[1024,256]{1,0:T(8,128)(2,1)}, bf16[1024,256]{1,0:T(8,128)(2,1)}, u32[]{:S(2)}, u32[]{:S(2)}) collective-permute-start(bf16[1024,256]{1,0:T(8,128)(2,1)} %pad_maximum_fusion.7), channel_id=1, source_target_pairs={{0,4},{2,6},{4,0},{6,2},{1,5},{3,7},{5,1},{7,3},{8,12},{10,14},{12... | collective-permute-start | bytes 1572872 | tf_op jit(solution)/shard_map/ppermute | solution.py:302
  74.0 28.0 %collective-permute-start.15 = (bf16[256,1024]{1,0:T(8,128)(2,1)}, bf16[256,1024]{1,0:T(8,128)(2,1)S(1)}, u32[]{:S(2)}, u32[]{:S(2)}) collective-permute-start(bf16[256,1024]{1,0:T(8,128)(2,1)} %collective-permute-done.14), channel_id=1, source_target_pairs={{0,8},{8,0},{16,24},{24,16},{1,9},{9,1},{17,25},{25,17},{2,10},{10... | collective-permute-start | bytes 1572872 | tf_op jit(solution)/shard_map/ppermute | solution.py:302
  76.6 82.9 %collective-permute-start.10 = (bf16[512,1024]{1,0:T(8,128)(2,1)}, bf16[512,1024]{1,0:T(8,128)(2,1)}, u32[]{:S(2)}, u32[]{:S(2)}) collective-permute-start(bf16[512,1024]{1,0:T(8,128)(2,1)} %pad_maximum_fusion.1.now_ref.refs_1_), channel_id=1, source_target_pairs={{0,8},{8,0},{16,24},{24,16},{1,9},{9,1},{17,25},{25,17},{2,10},{10... | collective-permute-start | bytes 3145736 | tf_op jit(solution)/shard_map/ppermute | solution.py:302
  98.0 66.0 %collective-permute-start.13 = (bf16[1024,512]{1,0:T(8,128)(2,1)}, bf16[1024,512]{1,0:T(8,128)(2,1)}, u32[]{:S(2)}, u32[]{:S(2)}) collective-permute-start(bf16[1024,512]{1,0:T(8,128)(2,1)} %pad_maximum_fusion.2.refs_1_.now_ref), channel_id=1, source_target_pairs={{0,8},{8,0},{16,24},{24,16},{1,9},{9,1},{17,25},{25,17},{2,10},{10... | collective-permute-start | bytes 3145736 | tf_op jit(solution)/shard_map/ppermute | solution.py:302
  98.8 45.1 %collective-permute-start.18 = (bf16[1024,256]{1,0:T(8,128)(2,1)}, bf16[1024,256]{1,0:T(8,128)(2,1)}, u32[]{:S(2)}, u32[]{:S(2)}) collective-permute-start(bf16[1024,256]{1,0:T(8,128)(2,1)} %collective-permute-done.17), channel_id=1, source_target_pairs={{0,8},{8,0},{16,24},{24,16},{1,9},{9,1},{17,25},{25,17},{2,10},{10... | collective-permute-start | bytes 1572872 | tf_op jit(solution)/shard_map/ppermute | solution.py:302
  101.9 27.8 %collective-permute-start.6 = (bf16[544,1024]{1,0:T(8,128)(2,1)}, bf16[544,1024]{1,0:T(8,128)(2,1)}, u32[]{:S(2)}, u32[]{:S(2)}) collective-permute-start(bf16[544,1024]{1,0:T(8,128)(2,1)} %constant_dynamic-update-slice_fusion.now_ref.refs_4_), channel_id=1, source_target_pairs={{0,16},{8,24},{16,0},{24,8},{1,17},{9,25},{17,1},{25,9},{2,18},{10... | collective-permute-start | bytes 3342344 | tf_op jit(solution)/shard_map/ppermute | solution.py:302
  105.0 50.1 %collective-permute-start.16 = (bf16[512,1024]{1,0:T(8,128)(2,1)}, bf16[512,1024]{1,0:T(8,128)(2,1)}, u32[]{:S(2)}, u32[]{:S(2)}) collective-permute-start(bf16[512,1024]{1,0:T(8,128)(2,1)} %constant_dynamic-update-slice_fusion.2.now_ref.refs_4_), channel_id=1, source_target_pairs={{0,16},{8,24},{16,0},{24,8},{1,17},{9,25},{17,1},{25,9},{2,18},{10... | collective-permute-start | bytes 3145736 | tf_op jit(solution)/shard_map/ppermute | solution.py:302
  141.7 7.3 %collective-permute-start.7 = (bf16[512,1024]{1,0:T(8,128)(2,1)S(1)}, bf16[512,1024]{1,0:T(8,128)(2,1)}, u32[]{:S(2)}, u32[]{:S(2)}) collective-permute-start(bf16[512,1024]{1,0:T(8,128)(2,1)S(1)} %shard_map.306.mine_ref), channel_id=1, source_target_pairs={{0,1},{1,0},{2,3},{3,2},{4,5},{5,4},{6,7},{7,6},{8,9},{9,8},{10,11... | collective-permute-start | bytes 3145736 | tf_op jit(solution)/shard_map/ppermute | solution.py:302
  145.8 26.1 %collective-permute-start.19 = (bf16[1024,512]{1,0:T(8,128)(2,1)}, bf16[1024,512]{1,0:T(8,128)(2,1)}, u32[]{:S(2)}, u32[]{:S(2)}) collective-permute-start(bf16[1024,512]{1,0:T(8,128)(2,1)} %constant_dynamic-update-slice_fusion.4.refs_4_.now_ref), channel_id=1, source_target_pairs={{0,16},{8,24},{16,0},{24,8},{1,17},{9,25},{17,1},{25,9},{2,18},{10... | collective-permute-start | bytes 3145736 | tf_op jit(solution)/shard_map/ppermute | solution.py:302
  164.0 12.8 %copy-start.8 = (bf16[512,1024]{1,0:T(8,128)(2,1)}, bf16[512,1024]{1,0:T(8,128)(2,1)S(1)}, u32[]{:S(2)}) copy-start(bf16[512,1024]{1,0:T(8,128)(2,1)S(1)} %get-tuple-element.70.refs_0_.left_ref) | copy-start | bytes 3145732
  176.8 3.9 %collective-permute-start.20 = (bf16[512,1024]{1,0:T(8,128)(2,1)S(1)}, bf16[512,1024]{1,0:T(8,128)(2,1)S(1)}, u32[]{:S(2)}, u32[]{:S(2)}) collective-permute-start(bf16[512,1024]{1,0:T(8,128)(2,1)S(1)} %shard_map.310.mine_ref), channel_id=1, source_target_pairs={{0,1},{1,0},{2,3},{3,2},{4,5},{5,4},{6,7},{7,6},{8,9},{9,8},{10,11... | collective-permute-start | bytes 3145736 | tf_op jit(solution)/shard_map/ppermute | solution.py:302
  176.9 3.3 collective-permute-start.21
  199.2 15.5 %collective-permute-start.22 = (bf16[512,1024]{1,0:T(8,128)(2,1)}, bf16[512,1024]{1,0:T(8,128)(2,1)}, u32[]{:S(2)}, u32[]{:S(2)}) collective-permute-start(bf16[512,1024]{1,0:T(8,128)(2,1)} %shard_map.314.mine_ref), channel_id=1, source_target_pairs={{0,1},{1,0},{2,3},{3,2},{4,5},{5,4},{6,7},{7,6},{8,9},{9,8},{10,11... | collective-permute-start | bytes 3145736 | tf_op jit(solution)/shard_map/ppermute | solution.py:302
  199.4 160.1 %copy-start.64 = (pred[2]{0:T(512)(128)(4,1)}, pred[2]{0:T(512)(128)(4,1)S(1)}, u32[]{:S(2)}) copy-start(pred[2]{0:T(512)(128)(4,1)S(1)} %iota_compare_fusion.3) | copy-start | bytes 10
  202.5 43.4 %collective-permute-start.36 = (bf16[1024,512]{1,0:T(8,128)(2,1)S(1)}, bf16[1024,512]{1,0:T(8,128)(2,1)S(1)}, u32[]{:S(2)}, u32[]{:S(2)}) collective-permute-start(bf16[1024,512]{1,0:T(8,128)(2,1)S(1)} %shard_map.331), channel_id=1, source_target_pairs={{0,16},{8,24},{16,0},{24,8},{1,17},{9,25},{17,1},{25,9},{2,18},{10... | collective-permute-start | bytes 3145736 | tf_op jit(solution)/shard_map/ppermute | solution.py:302
  205.3 41.4 %collective-permute-start.38 = (bf16[1024,512]{1,0:T(8,128)(2,1)S(1)}, bf16[1024,512]{1,0:T(8,128)(2,1)S(1)}, u32[]{:S(2)}, u32[]{:S(2)}) collective-permute-start(bf16[1024,512]{1,0:T(8,128)(2,1)S(1)} %shard_map.333), channel_id=1, source_target_pairs={{0,8},{8,0},{16,24},{24,16},{1,9},{9,1},{17,25},{25,17},{2,10},{10... | collective-permute-start | bytes 3145736 | tf_op jit(solution)/shard_map/ppermute | solution.py:302
  207.0 44.0 %collective-permute-start.30 = (bf16[512,1024]{1,0:T(8,128)(2,1)S(1)}, bf16[512,1024]{1,0:T(8,128)(2,1)S(1)}, u32[]{:S(2)}, u32[]{:S(2)}) collective-permute-start(bf16[512,1024]{1,0:T(8,128)(2,1)S(1)} %shard_map.327), channel_id=1, source_target_pairs={{0,16},{8,24},{16,0},{24,8},{1,17},{9,25},{17,1},{25,9},{2,18},{10... | collective-permute-start | bytes 3145736 | tf_op jit(solution)/shard_map/ppermute | solution.py:302
  209.1 44.7 %collective-permute-start.32 = (bf16[512,1024]{1,0:T(8,128)(2,1)S(1)}, bf16[512,1024]{1,0:T(8,128)(2,1)S(1)}, u32[]{:S(2)}, u32[]{:S(2)}) collective-permute-start(bf16[512,1024]{1,0:T(8,128)(2,1)S(1)} %shard_map.329), channel_id=1, source_target_pairs={{0,8},{8,0},{16,24},{24,16},{1,9},{9,1},{17,25},{25,17},{2,10},{10... | collective-permute-start | bytes 3145736 | tf_op jit(solution)/shard_map/ppermute | solution.py:302
  227.1 103.1 %collective-permute-start.24 = (bf16[544,1024]{1,0:T(8,128)(2,1)S(1)}, bf16[544,1024]{1,0:T(8,128)(2,1)S(1)}, u32[]{:S(2)}, u32[]{:S(2)}) collective-permute-start(bf16[544,1024]{1,0:T(8,128)(2,1)S(1)} %shard_map.322), channel_id=1, source_target_pairs={{0,16},{8,24},{16,0},{24,8},{1,17},{9,25},{17,1},{25,9},{2,18},{10... | collective-permute-start | bytes 3342344 | tf_op jit(solution)/shard_map/ppermute | solution.py:302
  245.9 85.1 %collective-permute-start.26 = (bf16[544,1024]{1,0:T(8,128)(2,1)S(1)}, bf16[544,1024]{1,0:T(8,128)(2,1)S(1)}, u32[]{:S(2)}, u32[]{:S(2)}) collective-permute-start(bf16[544,1024]{1,0:T(8,128)(2,1)S(1)} %shard_map.324), channel_id=1, source_target_pairs={{0,8},{8,0},{16,24},{24,16},{1,9},{9,1},{17,25},{25,17},{2,10},{10... | collective-permute-start | bytes 3342344 | tf_op jit(solution)/shard_map/ppermute | solution.py:302
  246.7 42.3 %collective-permute-start.37 = (bf16[1024,256]{1,0:T(8,128)(2,1)S(1)}, bf16[1024,256]{1,0:T(8,128)(2,1)S(1)}, u32[]{:S(2)}, u32[]{:S(2)}) collective-permute-start(bf16[1024,256]{1,0:T(8,128)(2,1)S(1)} %add_convert_fusion.12), channel_id=1, source_target_pairs={{0,8},{8,0},{16,24},{24,16},{1,9},{9,1},{17,25},{25,17},{2,10},{10... | collective-permute-start | bytes 1572872 | tf_op jit(solution)/shard_map/ppermute | solution.py:302
  251.0 38.7 %collective-permute-start.39 = (bf16[1024,256]{1,0:T(8,128)(2,1)S(1)}, bf16[1024,256]{1,0:T(8,128)(2,1)S(1)}, u32[]{:S(2)}, u32[]{:S(2)}) collective-permute-start(bf16[1024,256]{1,0:T(8,128)(2,1)S(1)} %add_convert_fusion.9), channel_id=1, source_target_pairs={{0,16},{8,24},{16,0},{24,8},{1,17},{9,25},{17,1},{25,9},{2,18},{10... | collective-permute-start | bytes 1572872 | tf_op jit(solution)/shard_map/ppermute | solution.py:302
  253.9 45.5 %collective-permute-start.31 = (bf16[256,1024]{1,0:T(8,128)(2,1)S(1)}, bf16[256,1024]{1,0:T(8,128)(2,1)S(1)}, u32[]{:S(2)}, u32[]{:S(2)}) collective-permute-start(bf16[256,1024]{1,0:T(8,128)(2,1)S(1)} %add_convert_fusion.19), channel_id=1, source_target_pairs={{0,8},{8,0},{16,24},{24,16},{1,9},{9,1},{17,25},{25,17},{2,10},{10... | collective-permute-start | bytes 1572872 | tf_op jit(solution)/shard_map/ppermute | solution.py:302
  289.0 13.1 %collective-permute-start.33 = (bf16[256,1024]{1,0:T(8,128)(2,1)S(1)}, bf16[256,1024]{1,0:T(8,128)(2,1)S(1)}, u32[]{:S(2)}, u32[]{:S(2)}) collective-permute-start(bf16[256,1024]{1,0:T(8,128)(2,1)S(1)} %add_convert_fusion.16), channel_id=1, source_target_pairs={{0,16},{8,24},{16,0},{24,8},{1,17},{9,25},{17,1},{25,9},{2,18},{10... | collective-permute-start | bytes 1572872 | tf_op jit(solution)/shard_map/ppermute | solution.py:302
  289.7 14.4 %collective-permute-start.23 = (bf16[256,1024]{1,0:T(8,128)(2,1)S(1)}, bf16[256,1024]{1,0:T(8,128)(2,1)S(1)}, u32[]{:S(2)}, u32[]{:S(2)}) collective-permute-start(bf16[256,1024]{1,0:T(8,128)(2,1)S(1)} %constant_dynamic-slice_fusion.6), channel_id=1, source_target_pairs={{0,1},{1,0},{2,3},{3,2},{4,5},{5,4},{6,7},{7,6},{8,9},{9,8},{10,11... | collective-permute-start | bytes 1572872 | tf_op jit(solution)/shard_map/ppermute | solution.py:302
  299.3 15.2 %collective-permute-start.40 = (bf16[1024,256]{1,0:T(8,128)(2,1)S(1)}, bf16[1024,256]{1,0:T(8,128)(2,1)S(1)}, u32[]{:S(2)}, u32[]{:S(2)}) collective-permute-start(bf16[1024,256]{1,0:T(8,128)(2,1)S(1)} %pad_maximum_fusion.12), channel_id=1, source_target_pairs={{0,2},{2,0},{4,6},{6,4},{1,3},{3,1},{5,7},{7,5},{8,10},{10,8},{12,... | collective-permute-start | bytes 1572872 | tf_op jit(solution)/shard_map/ppermute | solution.py:302
  302.5 27.5 %collective-permute-start.34 = (bf16[256,1024]{1,0:T(8,128)(2,1)S(1)}, bf16[256,1024]{1,0:T(8,128)(2,1)S(1)}, u32[]{:S(2)}, u32[]{:S(2)}) collective-permute-start(bf16[256,1024]{1,0:T(8,128)(2,1)S(1)} %pad_maximum_fusion.11), channel_id=1, source_target_pairs={{0,2},{2,0},{4,6},{6,4},{1,3},{3,1},{5,7},{7,5},{8,10},{10,8},{12,... | collective-permute-start | bytes 1572872 | tf_op jit(solution)/shard_map/ppermute | solution.py:302
  314.7 17.2 %collective-permute-start.41 = (bf16[512,256]{1,0:T(8,128)(2,1)S(1)}, bf16[512,256]{1,0:T(8,128)(2,1)S(1)}, u32[]{:S(2)}, u32[]{:S(2)}) collective-permute-start(bf16[512,256]{1,0:T(8,128)(2,1)S(1)} %slice.399), channel_id=1, source_target_pairs={{0,4},{2,6},{4,0},{6,2},{1,5},{3,7},{5,1},{7,3},{8,12},{10,14},{12... | collective-permute-start | bytes 786440 | tf_op jit(solution)/shard_map/ppermute | solution.py:302
  330.1 12.4 %collective-permute-start.35 = (bf16[256,512]{1,0:T(8,128)(2,1)S(1)}, bf16[256,512]{1,0:T(8,128)(2,1)S(1)}, u32[]{:S(2)}, u32[]{:S(2)}) collective-permute-start(bf16[256,512]{1,0:T(8,128)(2,1)S(1)} %slice.385), channel_id=1, source_target_pairs={{0,4},{2,6},{4,0},{6,2},{1,5},{3,7},{5,1},{7,3},{8,12},{10,14},{12... | collective-permute-start | bytes 786440 | tf_op jit(solution)/shard_map/ppermute | solution.py:302
  330.4 13.2 %collective-permute-start.25 = (bf16[272,1024]{1,0:T(8,128)(2,1)S(1)}, bf16[272,1024]{1,0:T(8,128)(2,1)S(1)}, u32[]{:S(2)}, u32[]{:S(2)}) collective-permute-start(bf16[272,1024]{1,0:T(8,128)(2,1)S(1)} %add_convert_fusion.5), channel_id=1, source_target_pairs={{0,8},{8,0},{16,24},{24,16},{1,9},{9,1},{17,25},{25,17},{2,10},{10... | collective-permute-start | bytes 1671176 | tf_op jit(solution)/shard_map/ppermute | solution.py:302
  331.2 13.0 %collective-permute-start.27 = (bf16[272,1024]{1,0:T(8,128)(2,1)S(1)}, bf16[272,1024]{1,0:T(8,128)(2,1)S(1)}, u32[]{:S(2)}, u32[]{:S(2)}) collective-permute-start(bf16[272,1024]{1,0:T(8,128)(2,1)S(1)} %add_convert_fusion.2), channel_id=1, source_target_pairs={{0,16},{8,24},{16,0},{24,8},{1,17},{9,25},{17,1},{25,9},{2,18},{10... | collective-permute-start | bytes 1671176 | tf_op jit(solution)/shard_map/ppermute | solution.py:302
  344.6 13.4 %collective-permute-start.28 = (bf16[272,1024]{1,0:T(8,128)(2,1)S(1)}, bf16[272,1024]{1,0:T(8,128)(2,1)S(1)}, u32[]{:S(2)}, u32[]{:S(2)}) collective-permute-start(bf16[272,1024]{1,0:T(8,128)(2,1)S(1)} %pad_maximum_fusion.4), channel_id=1, source_target_pairs={{0,2},{2,0},{4,6},{6,4},{1,3},{3,1},{5,7},{7,5},{8,10},{10,8},{12,... | collective-permute-start | bytes 1671176 | tf_op jit(solution)/shard_map/ppermute | solution.py:302
  358.3 13.2 %collective-permute-start.29 = (bf16[272,512]{1,0:T(8,128)(2,1)S(1)}, bf16[272,512]{1,0:T(8,128)(2,1)S(1)}, u32[]{:S(2)}, u32[]{:S(2)}) collective-permute-start(bf16[272,512]{1,0:T(8,128)(2,1)S(1)} %get-tuple-element.124), channel_id=1, source_target_pairs={{0,4},{2,6},{4,0},{6,2},{1,5},{3,7},{5,1},{7,3},{8,12},{10,14},{12... | collective-permute-start | bytes 835592 | tf_op jit(solution)/shard_map/ppermute | solution.py:302
  360.8 12.8 %copy-start.60 = (f32[6,256]{1,0:T(8,128)S(1)}, f32[6,256]{1,0:T(8,128)}, u32[]{:S(2)}) copy-start(f32[6,256]{1,0:T(8,128)} %param.23) | copy-start | bytes 18436
  360.8 12.8 %copy-start.61 = (f32[1,6,256]{2,0,1:T(1,128)S(1)}, f32[1,6,256]{2,0,1:T(1,128)}, u32[]{:S(2)}) copy-start(f32[1,6,256]{2,0,1:T(1,128)} %get-tuple-element.157) | copy-start | bytes 18436
  360.8 12.8 %copy-start.62 = (f32[1,6,256]{2,0,1:T(1,128)S(1)}, f32[1,6,256]{2,0,1:T(1,128)}, u32[]{:S(2)}) copy-start(f32[1,6,256]{2,0,1:T(1,128)} %get-tuple-element.158) | copy-start | bytes 18436
  (64 other events, 260.9 us)
where the time goes:
time: 378 us; the launch traced here: 376 us
  waiting for transfers between devices  184 us (49%)
  Pallas kernels  88 us (23%)
  starting transfers between devices  42.1 us (11%)
  local copies, waits for them, and re-layouts  32.8 us (9%)
  other arithmetic  27.2 us (7%)
    ppermute x42, waiting for transfers between devices, flip(): return lax.ppermute(value, axis, [(i, i ^ bit) for i in range(count)])  184 us
    ppermute x42, starting transfers between devices, flip(): return lax.ppermute(value, axis, [(i, i ^ bit) for i in range(count)])  42.1 us
    pallas_call x4, Pallas kernels, blend(): call(functools.partial(blend_kernel, weights, columns, dims), grid=(rows...  19 us
    unnamed x148, local copies, waits for them, and re-layouts  16.5 us
    pallas_call x4, Pallas kernels, project(): call(functools.partial(project_kernel, weight, gelu), grid=(width // tile...  16 us
    pallas_call x2, Pallas kernels, attend_back(): call(functools.partial(attend_back_kernel, per), grid=(blocks,), in_specs...  9.46 us
    pallas_call x8, Pallas kernels, block_grad(): call(block_grad_kernel, grid=(count,), in_specs=specs, out_specs=pl.Block...  9.08 us
    pallas_call x3, Pallas kernels, by_rows(): call(kernel, grid=(rows // tile,), in_specs=[spec(a.shape) for a in input...  8.68 us
  transfers between devices with their start and end apart: 42, of which 19 were waited for; matrix products, arithmetic and copies ran while one was open for 12% of the time, Pallas kernels for 17%

commit v1 on v0

--- a/solution.py
+++ b/solution.py
@@ -725,8 +725,23 @@
         arrays = gather_dp(block, order_e[c], 0)
         weight_e.append(Pieces(*arrays, order_e[c], part, part, 0))
     for c, block in enumerate(gather_z(own_r, 0)):
-        arrays = gather_dp(block, order_r[c], 1)
-        weight_r.append(Pieces(*arrays, order_r[c], part, part, 1))
+        if c == 0:
+            arrays = gather_dp(block, order_r[c], 1)
+            weight_r.append(Pieces(*arrays, order_r[c], part, part, 1))
+            continue
+        tall = block.shape[0] // 2
+        blocks = []
+        for n, order in enumerate((up, down)):
+            arrays = gather_dp(cut(block, n * tall, tall, 0), order, 1)
+            held = Pieces(*arrays, order, part, part, 1)
+            blocks.append(
+                [cut(arrays[held.where[j][0]], held.where[j][1], part, 1) for j in range(n_dp)]
+            )
+        sides = [
+            jnp.concatenate([jnp.concatenate([b[j] for j in js], 1) for b in blocks], 0)
+            for js in (range(n_dp // 2), range(n_dp // 2, n_dp))
+        ]
+        weight_r.append(Pieces(*sides, up, part, part, 1))
 
     vectors = jnp.concatenate([small_q[0][j][:6, :part] for j in range(n_dp)], 1)
     vectors = jnp.pad(vectors.astype(single), ((0, 2), (0, 0)))

time: 378 us -> 417 us (1.10)
  waiting for transfers between devices: 184 us -> 216 us
  other arithmetic: 27.2 us -> 33.1 us
  starting transfers between devices: 42.1 us -> 46.7 us
    ppermute x42 -> x44, waiting for transfers between devices: 184 us -> 216 us  [flip(): return lax.ppermute(value, axis, [(i, i ^ bit) for i in range(count)])]
    ppermute x42 -> x44, starting transfers between devices: 42.1 us -> 46.7 us  [flip(): return lax.ppermute(value, axis, [(i, i ^ bit) for i in range(count)])]
    unnamed x148 -> x173, local copies, waits for them, and re-layouts: 16.5 us -> 15 us
  transfers between devices with their start and end apart: 42 -> 44, of which waited for: 19 -> 23; matrix products, arithmetic and copies ran while one was open for 12% -> 11% of each run, Pallas kernels for 17% -> 16%
where the time goes in v1:
time: 417 us; the launch traced here: 415 us
  waiting for transfers between devices  216 us (52%)
  Pallas kernels  85.5 us (21%)
  starting transfers between devices  46.7 us (11%)
  other arithmetic  33.1 us (8%)
  local copies, waits for them, and re-layouts  31.4 us (8%)
    ppermute x44, waiting for transfers between devices, flip(): return lax.ppermute(value, axis, [(i, i ^ bit) for i in range(count)])  216 us
    ppermute x44, starting transfers between devices, flip(): return lax.ppermute(value, axis, [(i, i ^ bit) for i in range(count)])  46.7 us
    pallas_call x4, Pallas kernels, blend(): call(functools.partial(blend_kernel, weights, columns, dims), grid=(rows...  19.1 us
    pallas_call x4, Pallas kernels, project(): call(functools.partial(project_kernel, weight, gelu), grid=(width // tile...  15.6 us
    unnamed x173, local copies, waits for them, and re-layouts  15 us
    pallas_call x2, Pallas kernels, attend_back(): call(functools.partial(attend_back_kernel, per), grid=(blocks,), in_specs...  9.46 us
    pallas_call x8, Pallas kernels, block_grad(): call(block_grad_kernel, grid=(count,), in_specs=specs, out_specs=pl.Block...  8.96 us
    pallas_call x3, Pallas kernels, by_rows(): call(kernel, grid=(rows // tile,), in_specs=[spec(a.shape) for a in input...  8.53 us
  transfers between devices with their start and end apart: 44, of which 23 were waited for; matrix products, arithmetic and copies ran while one was open for 11% of the time, Pallas kernels for 16%

profile of v1, /device:TPU:0, one launch (start us, length us, event | category | flops | bytes accessed | tf_op | source)
XLA Modules:
  0.0 415.1 jit_solution(12207344648250444376)
XLA Ops:
  4.3 3.1 collective-permute-start.1
  8.5 6.4 %collective-permute-done.1 = bf16[272,512]{1,0:T(8,128)(2,1)S(1)} collective-permute-done((bf16[272,512]{1,0:T(8,128)(2,1)S(1)}, bf16[272,512]{1,0:T(8,128)(2,1)S(1)}, u32[]{:S(2)}, u32[]{:S(2)}) %collective-permute-start.1) | collective-permute-done | bytes 278560 | tf_op jit(solution)/shard_map/ppermute | solution.py:302
  15.8 1.9 collective-permute-start.2
  21.2 2.6 collective-permute-start.17
  26.0 5.9 %collective-permute-done.8 = bf16[256,512]{1,0:T(8,128)(2,1)S(1)} collective-permute-done((bf16[256,512]{1,0:T(8,128)(2,1)S(1)}, bf16[256,512]{1,0:T(8,128)(2,1)S(1)}, u32[]{:S(2)}, u32[]{:S(2)}) %collective-permute-start.8) | collective-permute-done | bytes 262176 | tf_op jit(solution)/shard_map/ppermute | solution.py:302
  36.8 34.8 %collective-permute-done.17 = bf16[1024,256]{1,0:T(8,128)(2,1)} collective-permute-done((bf16[1024,256]{1,0:T(8,128)(2,1)}, bf16[1024,256]{1,0:T(8,128)(2,1)}, u32[]{:S(2)}, u32[]{:S(2)}) %collective-permute-start.17) | collective-permute-done | bytes 524320 | tf_op jit(solution)/shard_map/ppermute | solution.py:302
  74.4 9.3 %collective-permute-done.4 = bf16[272,1024]{1,0:T(8,128)(2,1)} collective-permute-done((bf16[272,1024]{1,0:T(8,128)(2,1)}, bf16[272,1024]{1,0:T(8,128)(2,1)}, u32[]{:S(2)}, u32[]{:S(2)}) %collective-permute-start.4) | collective-permute-done | bytes 557088 | tf_op jit(solution)/shard_map/ppermute | solution.py:302
  87.3 6.9 %collective-permute-done.14 = bf16[256,1024]{1,0:T(8,128)(2,1)} collective-permute-done((bf16[256,1024]{1,0:T(8,128)(2,1)}, bf16[256,1024]{1,0:T(8,128)(2,1)}, u32[]{:S(2)}, u32[]{:S(2)}) %collective-permute-start.14) | collective-permute-done | bytes 524320 | tf_op jit(solution)/shard_map/ppermute | solution.py:302
  94.6 1.9 constant_dynamic-update-slice_fusion.3
  98.0 1.9 constant_dynamic-update-slice_fusion.1
  102.4 2.5 collective-permute-done.18
  108.3 1.9 constant_dynamic-update-slice_fusion.now_ref.refs_4_
  110.2 6.1 %collective-permute-done.15 = bf16[256,1024]{1,0:T(8,128)(2,1)} collective-permute-done((bf16[256,1024]{1,0:T(8,128)(2,1)}, bf16[256,1024]{1,0:T(8,128)(2,1)}, u32[]{:S(2)}, u32[]{:S(2)}) %collective-permute-start.15) | collective-permute-done | bytes 524320 | tf_op jit(solution)/shard_map/ppermute | solution.py:302
  122.5 3.6 shard_map.302.q_ref.k_ref.v_ref
  126.1 3.0 shard_map.303
  130.9 19.4 %collective-permute-done.6.other_ref.refs_5_ = bf16[544,1024]{1,0:T(8,128)(2,1)} collective-permute-done((bf16[544,1024]{1,0:T(8,128)(2,1)}, bf16[544,1024]{1,0:T(8,128)(2,1)}, u32[]{:S(2)}, u32[]{:S(2)}) %collective-permute-start.6) | collective-permute-done | bytes 1114144 | tf_op jit(solution)/shard_map/ppermute | solution.py:302
  153.4 3.5 shard_map.304.q_ref.k_ref.v_ref
  157.0 3.0 shard_map.305
  160.0 4.5 %shard_map.306.mine_ref = bf16[512,1024]{1,0:T(8,128)(2,1)} custom-call(bf16[512,256]{1,0:T(8,128)(2,1)S(1)} %get-tuple-element.62.refs_0_.heads_ref, bf16[544,1024]{1,0:T(8,128)(2,1)S(1)} %pad_maximum_fusion.now_ref.refs_1_, bf16[544,1024]{1,0:T(8,128)(2,1)} %collective-permute-done.3.other_ref.refs_2_, ...), custom_call_target="tpu_custom_call" | custom-call | flops 536870912 | bytes 4194304 | tf_op jit(solution)/shard_map/pallas_call | solution.py:442
  164.7 2.1 pad_maximum_fusion.1.now_ref.refs_1_
  168.4 2.1 pad_maximum_fusion.2.refs_1_.now_ref
  173.9 2.1 maximum_maximum_fusion.1.refs_5_.other_ref
  179.2 2.9 shard_map.307
  184.1 4.4 %shard_map.309 = (bf16[512,1024]{1,0:T(8,128)(2,1)S(1)}, f32[512,1024]{1,0:T(8,128)S(1)}) custom-call(bf16[512,1024]{1,0:T(8,128)(2,1)S(1)} %get-tuple-element.69.x_ref.left_ref, bf16[512,1024]{1,0:T(8,128)(2,1)} %constant_dynamic-update-slice_fusion.2.now_ref.refs_4_, bf16[512,1024]{1,0:T(8,128)(2,1)} %collective-permute-done.16.other_ref.refs_5_, ...), custom_call_target="tpu_custom_call" | custom-call | flops 1073741824 | bytes 2097152 | tf_op jit(solution)/shard_map/pallas_call | solution.py:372
  188.5 4.8 %collective-permute-done.10.other_ref.refs_2_ = bf16[512,1024]{1,0:T(8,128)(2,1)} collective-permute-done((bf16[512,1024]{1,0:T(8,128)(2,1)}, bf16[512,1024]{1,0:T(8,128)(2,1)}, u32[]{:S(2)}, u32[]{:S(2)}) %collective-permute-start.10) | collective-permute-done | bytes 1048608 | tf_op jit(solution)/shard_map/ppermute | solution.py:302
  193.2 4.0 shard_map.308
  197.3 17.9 %collective-permute-done.13.refs_2_.other_ref = bf16[1024,512]{1,0:T(8,128)(2,1)} collective-permute-done((bf16[1024,512]{1,0:T(8,128)(2,1)}, bf16[1024,512]{1,0:T(8,128)(2,1)}, u32[]{:S(2)}, u32[]{:S(2)}) %collective-permute-start.13) | collective-permute-done | bytes 1048608 | tf_op jit(solution)/shard_map/ppermute | solution.py:302
  215.2 4.1 shard_map.310.mine_ref
  220.8 2.1 collective-permute-done.23
  223.4 2.3 shard_map.311
  227.1 2.2 shard_map.313
  229.4 4.1 shard_map.312
  234.1 5.9 %shard_map.314.mine_ref = bf16[512,1024]{1,0:T(8,128)(2,1)} custom-call(bf16[512,1024]{1,0:T(8,128)(2,1)S(1)} %get-tuple-element.77.refs_0_.right_ref, bf16[512,1024]{1,0:T(8,128)(2,1)} %pad_maximum_fusion.1.now_ref.refs_1_, bf16[512,1024]{1,0:T(8,128)(2,1)} %collective-permute-done.10.other_ref.refs_2_, ...), custom_call_target="tpu_custom_call" | custom-call | flops 2147483648 | bytes 4194304 | tf_op jit(solution)/shard_map/pallas_call | solution.py:442
  256.1 3.4 shard_map.315
  259.5 2.1 shard_map.316.up_ref
  261.6 4.7 %shard_map.317 = (bf16[512,1024]{1,0:T(8,128)(2,1)S(1)}, f32[8,1024]{1,0:T(8,128)S(1)}) custom-call(bf16[512,1024]{1,0:T(8,128)(2,1)S(1)} %copy-done.3, bf16[512,1024]{1,0:T(8,128)(2,1)S(1)} %copy-done.3, bf16[512,1024]{1,0:T(8,128)(2,1)S(1)} %copy-done.3, bf16[512,256]{1,0:T(8,128)(2,1)S(1)} %shard_map.316.up_ref, f32[512,256]{1,0:T(8,128)S(1)} %copy-done.38, ...), custom_call_target="tpu_custom_call" | custom-call | flops 1342177280 | bytes 3145728 | tf_op jit(solution)/shard_map/pallas_call | solution.py:142
  268.3 2.3 shard_map.318.up_ref
  270.6 4.7 %shard_map.319 = (bf16[512,1024]{1,0:T(8,128)(2,1)S(1)}, f32[8,1024]{1,0:T(8,128)S(1)}) custom-call(bf16[512,1024]{1,0:T(8,128)(2,1)S(1)} %copy-done.5, bf16[512,1024]{1,0:T(8,128)(2,1)S(1)} %copy-done.5, bf16[512,1024]{1,0:T(8,128)(2,1)S(1)} %copy-done.5, bf16[512,256]{1,0:T(8,128)(2,1)S(1)} %shard_map.318.up_ref, f32[512,256]{1,0:T(8,128)S(1)} %copy-done.40, ...), custom_call_target="tpu_custom_call" | custom-call | flops 1342177280 | bytes 3145728 | tf_op jit(solution)/shard_map/pallas_call | solution.py:142
  276.6 4.6 %shard_map.320 = bf16[512,1024]{1,0:T(8,128)(2,1)S(1)} custom-call(bf16[512,1024]{1,0:T(8,128)(2,1)S(1)} %get-tuple-element.89.refs_0_.stack_ref, bf16[544,1024]{1,0:T(8,128)(2,1)S(1)} %pad_maximum_fusion.now_ref.refs_1_, bf16[544,1024]{1,0:T(8,128)(2,1)} %collective-permute-done.3.other_ref.refs_2_, ...), custom_call_target="tpu_custom_call" | custom-call | flops 2147483648 | bytes 4194304 | tf_op jit(solution)/shard_map/pallas_call | solution.py:442
  287.8 4.0 collective-permute-done.32
  295.3 33.4 %collective-permute-done.39 = bf16[1024,256]{1,0:T(8,128)(2,1)S(1)} collective-permute-done((bf16[1024,256]{1,0:T(8,128)(2,1)S(1)}, bf16[1024,256]{1,0:T(8,128)(2,1)S(1)}, u32[]{:S(2)}, u32[]{:S(2)}) %collective-permute-start.39) | collective-permute-done | bytes 524320 | tf_op jit(solution)/shard_map/ppermute | solution.py:302
  330.9 8.2 %collective-permute-done.33 = bf16[256,1024]{1,0:T(8,128)(2,1)S(1)} collective-permute-done((bf16[256,1024]{1,0:T(8,128)(2,1)S(1)}, bf16[256,1024]{1,0:T(8,128)(2,1)S(1)}, u32[]{:S(2)}, u32[]{:S(2)}) %collective-permute-start.33) | collective-permute-done | bytes 524320 | tf_op jit(solution)/shard_map/ppermute | solution.py:302
  343.1 10.8 %collective-permute-done.42 = bf16[1024,256]{1,0:T(8,128)(2,1)S(1)} collective-permute-done((bf16[1024,256]{1,0:T(8,128)(2,1)S(1)}, bf16[1024,256]{1,0:T(8,128)(2,1)S(1)}, u32[]{:S(2)}, u32[]{:S(2)}) %collective-permute-start.42) | collective-permute-done | bytes 524320 | tf_op jit(solution)/shard_map/ppermute | solution.py:302
  355.5 13.5 %collective-permute-done.36 = bf16[256,1024]{1,0:T(8,128)(2,1)S(1)} collective-permute-done((bf16[256,1024]{1,0:T(8,128)(2,1)S(1)}, bf16[256,1024]{1,0:T(8,128)(2,1)S(1)}, u32[]{:S(2)}, u32[]{:S(2)}) %collective-permute-start.36) | collective-permute-done | bytes 524320 | tf_op jit(solution)/shard_map/ppermute | solution.py:302
  374.7 7.6 %collective-permute-done.37 = bf16[256,512]{1,0:T(8,128)(2,1)S(1)} collective-permute-done((bf16[256,512]{1,0:T(8,128)(2,1)S(1)}, bf16[256,512]{1,0:T(8,128)(2,1)S(1)}, u32[]{:S(2)}, u32[]{:S(2)}) %collective-permute-start.37) | collective-permute-done | bytes 262176 | tf_op jit(solution)/shard_map/ppermute | solution.py:302
  384.7 2.5 collective-permute-start.30
  389.6 8.1 %collective-permute-done.30 = bf16[272,1024]{1,0:T(8,128)(2,1)S(1)} collective-permute-done((bf16[272,1024]{1,0:T(8,128)(2,1)S(1)}, bf16[272,1024]{1,0:T(8,128)(2,1)S(1)}, u32[]{:S(2)}, u32[]{:S(2)}) %collective-permute-start.30) | collective-permute-done | bytes 557088 | tf_op jit(solution)/shard_map/ppermute | solution.py:302
  400.3 10.1 %collective-permute-done.31.other_ref = bf16[272,512]{1,0:T(8,128)(2,1)S(1)} collective-permute-done((bf16[272,512]{1,0:T(8,128)(2,1)S(1)}, bf16[272,512]{1,0:T(8,128)(2,1)S(1)}, u32[]{:S(2)}, u32[]{:S(2)}) %collective-permute-start.31) | collective-permute-done | bytes 278560 | tf_op jit(solution)/shard_map/ppermute | solution.py:302
  (384 shorter events, 109.5 us)
Async XLA Ops:
  4.3 10.6 %collective-permute-start.1 = (bf16[272,512]{1,0:T(8,128)(2,1)S(1)}, bf16[272,512]{1,0:T(8,128)(2,1)S(1)}, u32[]{:S(2)}, u32[]{:S(2)}) collective-permute-start(bf16[272,512]{1,0:T(8,128)(2,1)S(1)} %pad_maximum_fusion.15), channel_id=1, source_target_pairs={{0,2},{2,0},{4,6},{6,4},{1,3},{3,1},{5,7},{7,5},{8,10},{10,8},{12,... | collective-permute-start | bytes 835592 | tf_op jit(solution)/shard_map/ppermute | solution.py:302
  7.5 12.8 %collective-permute-start.11 = (bf16[512,256]{1,0:T(8,128)(2,1)S(1)}, bf16[512,256]{1,0:T(8,128)(2,1)S(1)}, u32[]{:S(2)}, u32[]{:S(2)}) collective-permute-start(bf16[512,256]{1,0:T(8,128)(2,1)S(1)} %convert_element_type.265), channel_id=1, source_target_pairs={{0,2},{2,0},{4,6},{6,4},{1,3},{3,1},{5,7},{7,5},{8,10},{10,8},{12,... | collective-permute-start | bytes 786440 | tf_op jit(solution)/shard_map/ppermute | solution.py:302
  15.8 18.2 %collective-permute-start.2 = (bf16[272,1024]{1,0:T(8,128)(2,1)}, bf16[272,1024]{1,0:T(8,128)(2,1)}, u32[]{:S(2)}, u32[]{:S(2)}) collective-permute-start(bf16[272,1024]{1,0:T(8,128)(2,1)} %pad_maximum_fusion.3), channel_id=1, source_target_pairs={{0,8},{8,0},{16,24},{24,16},{1,9},{9,1},{17,25},{25,17},{2,10},{10... | collective-permute-start | bytes 1671176 | tf_op jit(solution)/shard_map/ppermute | solution.py:302
  18.6 66.0 %collective-permute-start = (bf16[256,1024]{1,0:T(8,128)(2,1)}, bf16[256,1024]{1,0:T(8,128)(2,1)}, u32[]{:S(2)}, u32[]{:S(2)}) collective-permute-start(bf16[256,1024]{1,0:T(8,128)(2,1)} %pad_maximum_fusion.5), channel_id=1, source_target_pairs={{0,1},{1,0},{2,3},{3,2},{4,5},{5,4},{6,7},{7,6},{8,9},{9,8},{10,11... | collective-permute-start | bytes 1572872 | tf_op jit(solution)/shard_map/ppermute | solution.py:302
  18.7 13.2 %collective-permute-start.8 = (bf16[256,512]{1,0:T(8,128)(2,1)S(1)}, bf16[256,512]{1,0:T(8,128)(2,1)S(1)}, u32[]{:S(2)}, u32[]{:S(2)}) collective-permute-start(bf16[256,512]{1,0:T(8,128)(2,1)S(1)} %convert_element_type.264), channel_id=1, source_target_pairs={{0,2},{2,0},{4,6},{6,4},{1,3},{3,1},{5,7},{7,5},{8,10},{10,8},{12,... | collective-permute-start | bytes 786440 | tf_op jit(solution)/shard_map/ppermute | solution.py:302
  21.2 50.5 %collective-permute-start.17 = (bf16[1024,256]{1,0:T(8,128)(2,1)}, bf16[1024,256]{1,0:T(8,128)(2,1)}, u32[]{:S(2)}, u32[]{:S(2)}) collective-permute-start(bf16[1024,256]{1,0:T(8,128)(2,1)} %pad_maximum_fusion.7), channel_id=1, source_target_pairs={{0,4},{2,6},{4,0},{6,2},{1,5},{3,7},{5,1},{7,3},{8,12},{10,14},{12... | collective-permute-start | bytes 1572872 | tf_op jit(solution)/shard_map/ppermute | solution.py:302
  25.6 58.1 %collective-permute-start.4 = (bf16[272,1024]{1,0:T(8,128)(2,1)}, bf16[272,1024]{1,0:T(8,128)(2,1)}, u32[]{:S(2)}, u32[]{:S(2)}) collective-permute-start(bf16[272,1024]{1,0:T(8,128)(2,1)} %pad_maximum_fusion.3), channel_id=1, source_target_pairs={{0,4},{2,6},{4,0},{6,2},{1,5},{3,7},{5,1},{7,3},{8,12},{10,14},{12... | collective-permute-start | bytes 1671176 | tf_op jit(solution)/shard_map/ppermute | solution.py:302
  31.9 40.9 %copy-start.63 = (bf16[256,512]{1,0:T(8,128)(2,1)}, bf16[256,512]{1,0:T(8,128)(2,1)S(1)}, u32[]{:S(2)}) copy-start(bf16[256,512]{1,0:T(8,128)(2,1)S(1)} %collective-permute-done.8) | copy-start | bytes 786436
  32.7 61.4 %collective-permute-start.14 = (bf16[256,1024]{1,0:T(8,128)(2,1)}, bf16[256,1024]{1,0:T(8,128)(2,1)}, u32[]{:S(2)}, u32[]{:S(2)}) collective-permute-start(bf16[256,1024]{1,0:T(8,128)(2,1)} %pad_maximum_fusion.6), channel_id=1, source_target_pairs={{0,4},{2,6},{4,0},{6,2},{1,5},{3,7},{5,1},{7,3},{8,12},{10,14},{12... | collective-permute-start | bytes 1572872 | tf_op jit(solution)/shard_map/ppermute | solution.py:302
  35.2 85.2 %collective-permute-start.3 = (bf16[544,1024]{1,0:T(8,128)(2,1)S(1)}, bf16[544,1024]{1,0:T(8,128)(2,1)}, u32[]{:S(2)}, u32[]{:S(2)}) collective-permute-start(bf16[544,1024]{1,0:T(8,128)(2,1)S(1)} %pad_maximum_fusion.now_ref.refs_1_), channel_id=1, source_target_pairs={{0,16},{8,24},{16,0},{24,8},{1,17},{9,25},{17,1},{25,9},{2,18},{10... | collective-permute-start | bytes 3342344 | tf_op jit(solution)/shard_map/ppermute | solution.py:302
  72.8 33.7 %copy-start.47 = (bf16[512,256]{1,0:T(8,128)(2,1)}, bf16[512,256]{1,0:T(8,128)(2,1)S(1)}, u32[]{:S(2)}) copy-start(bf16[512,256]{1,0:T(8,128)(2,1)S(1)} %get-tuple-element.152) | copy-start | bytes 786436
  72.8 27.2 %collective-permute-start.19 = (bf16[512,256]{1,0:T(8,128)(2,1)S(1)}, bf16[512,256]{1,0:T(8,128)(2,1)S(1)}, u32[]{:S(2)}, u32[]{:S(2)}) collective-permute-start(bf16[512,256]{1,0:T(8,128)(2,1)S(1)} %get-tuple-element.153), channel_id=1, source_target_pairs={{0,16},{8,24},{16,0},{24,8},{1,17},{9,25},{17,1},{25,9},{2,18},{10... | collective-permute-start | bytes 786440 | tf_op jit(solution)/shard_map/ppermute | solution.py:302
  83.6 23.7 %collective-permute-start.5 = (bf16[272,1024]{1,0:T(8,128)(2,1)}, bf16[272,1024]{1,0:T(8,128)(2,1)}, u32[]{:S(2)}, u32[]{:S(2)}) collective-permute-start(bf16[272,1024]{1,0:T(8,128)(2,1)} %collective-permute-done.4), channel_id=1, source_target_pairs={{0,8},{8,0},{16,24},{24,16},{1,9},{9,1},{17,25},{25,17},{2,10},{10... | collective-permute-start | bytes 1671176 | tf_op jit(solution)/shard_map/ppermute | solution.py:302
  86.2 18.8 %collective-permute-start.18 = (bf16[512,256]{1,0:T(8,128)(2,1)S(1)}, bf16[512,256]{1,0:T(8,128)(2,1)S(1)}, u32[]{:S(2)}, u32[]{:S(2)}) collective-permute-start(bf16[512,256]{1,0:T(8,128)(2,1)S(1)} %get-tuple-element.152), channel_id=1, source_target_pairs={{0,8},{8,0},{16,24},{24,16},{1,9},{9,1},{17,25},{25,17},{2,10},{10... | collective-permute-start | bytes 786440 | tf_op jit(solution)/shard_map/ppermute | solution.py:302
  94.1 22.2 %collective-permute-start.15 = (bf16[256,1024]{1,0:T(8,128)(2,1)}, bf16[256,1024]{1,0:T(8,128)(2,1)}, u32[]{:S(2)}, u32[]{:S(2)}) collective-permute-start(bf16[256,1024]{1,0:T(8,128)(2,1)} %collective-permute-done.14), channel_id=1, source_target_pairs={{0,8},{8,0},{16,24},{24,16},{1,9},{9,1},{17,25},{25,17},{2,10},{10... | collective-permute-start | bytes 1572872 | tf_op jit(solution)/shard_map/ppermute | solution.py:302
  100.0 64.6 %collective-permute-start.9 = (bf16[256,1024]{1,0:T(8,128)(2,1)}, bf16[256,1024]{1,0:T(8,128)(2,1)}, u32[]{:S(2)}, u32[]{:S(2)}) collective-permute-start(bf16[256,1024]{1,0:T(8,128)(2,1)} %pad_maximum_fusion.6), channel_id=1, source_target_pairs={{0,16},{8,24},{16,0},{24,8},{1,17},{9,25},{17,1},{25,9},{2,18},{10... | collective-permute-start | bytes 1572872 | tf_op jit(solution)/shard_map/ppermute | solution.py:302
  104.9 61.9 %collective-permute-start.12 = (bf16[1024,256]{1,0:T(8,128)(2,1)}, bf16[1024,256]{1,0:T(8,128)(2,1)}, u32[]{:S(2)}, u32[]{:S(2)}) collective-permute-start(bf16[1024,256]{1,0:T(8,128)(2,1)} %pad_maximum_fusion.7), channel_id=1, source_target_pairs={{0,16},{8,24},{16,0},{24,8},{1,17},{9,25},{17,1},{25,9},{2,18},{10... | collective-permute-start | bytes 1572872 | tf_op jit(solution)/shard_map/ppermute | solution.py:302
  107.3 63.9 %collective-permute-start.20 = (bf16[512,512]{1,0:T(8,128)(2,1)}, bf16[512,512]{1,0:T(8,128)(2,1)}, u32[]{:S(2)}, u32[]{:S(2)}) collective-permute-start(bf16[512,512]{1,0:T(8,128)(2,1)} %pad_maximum_fusion.9), channel_id=1, source_target_pairs={{0,8},{8,0},{16,24},{24,16},{1,9},{9,1},{17,25},{25,17},{2,10},{10... | collective-permute-start | bytes 1572872 | tf_op jit(solution)/shard_map/ppermute | solution.py:302
  116.3 34.0 %collective-permute-start.6 = (bf16[544,1024]{1,0:T(8,128)(2,1)}, bf16[544,1024]{1,0:T(8,128)(2,1)}, u32[]{:S(2)}, u32[]{:S(2)}) collective-permute-start(bf16[544,1024]{1,0:T(8,128)(2,1)} %constant_dynamic-update-slice_fusion.now_ref.refs_4_), channel_id=1, source_target_pairs={{0,16},{8,24},{16,0},{24,8},{1,17},{9,25},{17,1},{25,9},{2,18},{10... | collective-permute-start | bytes 3342344 | tf_op jit(solution)/shard_map/ppermute | solution.py:302
  120.4 53.5 %collective-permute-start.21 = (bf16[512,512]{1,0:T(8,128)(2,1)}, bf16[512,512]{1,0:T(8,128)(2,1)}, u32[]{:S(2)}, u32[]{:S(2)}) collective-permute-start(bf16[512,512]{1,0:T(8,128)(2,1)} %pad_maximum_fusion.8), channel_id=1, source_target_pairs={{0,16},{8,24},{16,0},{24,8},{1,17},{9,25},{17,1},{25,9},{2,18},{10... | collective-permute-start | bytes 1572872 | tf_op jit(solution)/shard_map/ppermute | solution.py:302
  150.3 33.8 %collective-permute-start.16 = (bf16[512,1024]{1,0:T(8,128)(2,1)}, bf16[512,1024]{1,0:T(8,128)(2,1)}, u32[]{:S(2)}, u32[]{:S(2)}) collective-permute-start(bf16[512,1024]{1,0:T(8,128)(2,1)} %constant_dynamic-update-slice_fusion.2.now_ref.refs_4_), channel_id=1, source_target_pairs={{0,16},{8,24},{16,0},{24,8},{1,17},{9,25},{17,1},{25,9},{2,18},{10... | collective-permute-start | bytes 3145736 | tf_op jit(solution)/shard_map/ppermute | solution.py:302
  164.6 12.4 %collective-permute-start.7 = (bf16[512,1024]{1,0:T(8,128)(2,1)}, bf16[512,1024]{1,0:T(8,128)(2,1)S(1)}, u32[]{:S(2)}, u32[]{:S(2)}) collective-permute-start(bf16[512,1024]{1,0:T(8,128)(2,1)} %shard_map.306.mine_ref), channel_id=1, source_target_pairs={{0,1},{1,0},{2,3},{3,2},{4,5},{5,4},{6,7},{7,6},{8,9},{9,8},{10,11... | collective-permute-start | bytes 3145736 | tf_op jit(solution)/shard_map/ppermute | solution.py:302
  166.8 26.4 %collective-permute-start.10 = (bf16[512,1024]{1,0:T(8,128)(2,1)}, bf16[512,1024]{1,0:T(8,128)(2,1)}, u32[]{:S(2)}, u32[]{:S(2)}) collective-permute-start(bf16[512,1024]{1,0:T(8,128)(2,1)} %pad_maximum_fusion.1.now_ref.refs_1_), channel_id=1, source_target_pairs={{0,8},{8,0},{16,24},{24,16},{1,9},{9,1},{17,25},{25,17},{2,10},{10... | collective-permute-start | bytes 3145736 | tf_op jit(solution)/shard_map/ppermute | solution.py:302
  171.2 44.0 %collective-permute-start.13 = (bf16[1024,512]{1,0:T(8,128)(2,1)}, bf16[1024,512]{1,0:T(8,128)(2,1)}, u32[]{:S(2)}, u32[]{:S(2)}) collective-permute-start(bf16[1024,512]{1,0:T(8,128)(2,1)} %pad_maximum_fusion.2.refs_1_.now_ref), channel_id=1, source_target_pairs={{0,8},{8,0},{16,24},{24,16},{1,9},{9,1},{17,25},{25,17},{2,10},{10... | collective-permute-start | bytes 3145736 | tf_op jit(solution)/shard_map/ppermute | solution.py:302
  188.4 30.9 %copy-start.6 = (bf16[512,1024]{1,0:T(8,128)(2,1)}, bf16[512,1024]{1,0:T(8,128)(2,1)S(1)}, u32[]{:S(2)}) copy-start(bf16[512,1024]{1,0:T(8,128)(2,1)S(1)} %get-tuple-element.71.refs_3_.left_ref) | copy-start | bytes 3145732
  219.4 3.9 collective-permute-start.22
  219.6 3.3 collective-permute-start.23
  240.0 15.4 %collective-permute-start.24 = (bf16[512,1024]{1,0:T(8,128)(2,1)}, bf16[512,1024]{1,0:T(8,128)(2,1)}, u32[]{:S(2)}, u32[]{:S(2)}) collective-permute-start(bf16[512,1024]{1,0:T(8,128)(2,1)} %shard_map.314.mine_ref), channel_id=1, source_target_pairs={{0,1},{1,0},{2,3},{3,2},{4,5},{5,4},{6,7},{7,6},{8,9},{9,8},{10,11... | collective-permute-start | bytes 3145736 | tf_op jit(solution)/shard_map/ppermute | solution.py:302
  240.2 158.8 %copy-start.77 = (pred[2]{0:T(512)(128)(4,1)}, pred[2]{0:T(512)(128)(4,1)S(1)}, u32[]{:S(2)}) copy-start(pred[2]{0:T(512)(128)(4,1)S(1)} %iota_compare_fusion.3) | copy-start | bytes 10
  243.2 42.1 %collective-permute-start.38 = (bf16[1024,512]{1,0:T(8,128)(2,1)S(1)}, bf16[1024,512]{1,0:T(8,128)(2,1)S(1)}, u32[]{:S(2)}, u32[]{:S(2)}) collective-permute-start(bf16[1024,512]{1,0:T(8,128)(2,1)S(1)} %shard_map.331), channel_id=1, source_target_pairs={{0,16},{8,24},{16,0},{24,8},{1,17},{9,25},{17,1},{25,9},{2,18},{10... | collective-permute-start | bytes 3145736 | tf_op jit(solution)/shard_map/ppermute | solution.py:302
  245.0 42.0 %collective-permute-start.40 = (bf16[1024,512]{1,0:T(8,128)(2,1)S(1)}, bf16[1024,512]{1,0:T(8,128)(2,1)S(1)}, u32[]{:S(2)}, u32[]{:S(2)}) collective-permute-start(bf16[1024,512]{1,0:T(8,128)(2,1)S(1)} %shard_map.333), channel_id=1, source_target_pairs={{0,8},{8,0},{16,24},{24,16},{1,9},{9,1},{17,25},{25,17},{2,10},{10... | collective-permute-start | bytes 3145736 | tf_op jit(solution)/shard_map/ppermute | solution.py:302
  247.7 44.2 %collective-permute-start.32 = (bf16[512,1024]{1,0:T(8,128)(2,1)S(1)}, bf16[512,1024]{1,0:T(8,128)(2,1)S(1)}, u32[]{:S(2)}, u32[]{:S(2)}) collective-permute-start(bf16[512,1024]{1,0:T(8,128)(2,1)S(1)} %shard_map.327), channel_id=1, source_target_pairs={{0,16},{8,24},{16,0},{24,8},{1,17},{9,25},{17,1},{25,9},{2,18},{10... | collective-permute-start | bytes 3145736 | tf_op jit(solution)/shard_map/ppermute | solution.py:302
  250.3 43.3 %collective-permute-start.34 = (bf16[512,1024]{1,0:T(8,128)(2,1)S(1)}, bf16[512,1024]{1,0:T(8,128)(2,1)S(1)}, u32[]{:S(2)}, u32[]{:S(2)}) collective-permute-start(bf16[512,1024]{1,0:T(8,128)(2,1)S(1)} %shard_map.329), channel_id=1, source_target_pairs={{0,8},{8,0},{16,24},{24,16},{1,9},{9,1},{17,25},{25,17},{2,10},{10... | collective-permute-start | bytes 3145736 | tf_op jit(solution)/shard_map/ppermute | solution.py:302
  267.7 102.5 %collective-permute-start.26 = (bf16[544,1024]{1,0:T(8,128)(2,1)S(1)}, bf16[544,1024]{1,0:T(8,128)(2,1)S(1)}, u32[]{:S(2)}, u32[]{:S(2)}) collective-permute-start(bf16[544,1024]{1,0:T(8,128)(2,1)S(1)} %shard_map.322), channel_id=1, source_target_pairs={{0,16},{8,24},{16,0},{24,8},{1,17},{9,25},{17,1},{25,9},{2,18},{10... | collective-permute-start | bytes 3342344 | tf_op jit(solution)/shard_map/ppermute | solution.py:302
  285.4 86.2 %collective-permute-start.28 = (bf16[544,1024]{1,0:T(8,128)(2,1)S(1)}, bf16[544,1024]{1,0:T(8,128)(2,1)S(1)}, u32[]{:S(2)}, u32[]{:S(2)}) collective-permute-start(bf16[544,1024]{1,0:T(8,128)(2,1)S(1)} %shard_map.324), channel_id=1, source_target_pairs={{0,8},{8,0},{16,24},{24,16},{1,9},{9,1},{17,25},{25,17},{2,10},{10... | collective-permute-start | bytes 3342344 | tf_op jit(solution)/shard_map/ppermute | solution.py:302
  287.0 41.7 %collective-permute-start.39 = (bf16[1024,256]{1,0:T(8,128)(2,1)S(1)}, bf16[1024,256]{1,0:T(8,128)(2,1)S(1)}, u32[]{:S(2)}, u32[]{:S(2)}) collective-permute-start(bf16[1024,256]{1,0:T(8,128)(2,1)S(1)} %add_convert_fusion.12), channel_id=1, source_target_pairs={{0,8},{8,0},{16,24},{24,16},{1,9},{9,1},{17,25},{25,17},{2,10},{10... | collective-permute-start | bytes 1572872 | tf_op jit(solution)/shard_map/ppermute | solution.py:302
  291.8 38.6 %collective-permute-start.41 = (bf16[1024,256]{1,0:T(8,128)(2,1)S(1)}, bf16[1024,256]{1,0:T(8,128)(2,1)S(1)}, u32[]{:S(2)}, u32[]{:S(2)}) collective-permute-start(bf16[1024,256]{1,0:T(8,128)(2,1)S(1)} %add_convert_fusion.9), channel_id=1, source_target_pairs={{0,16},{8,24},{16,0},{24,8},{1,17},{9,25},{17,1},{25,9},{2,18},{10... | collective-permute-start | bytes 1572872 | tf_op jit(solution)/shard_map/ppermute | solution.py:302
  293.6 45.5 %collective-permute-start.33 = (bf16[256,1024]{1,0:T(8,128)(2,1)S(1)}, bf16[256,1024]{1,0:T(8,128)(2,1)S(1)}, u32[]{:S(2)}, u32[]{:S(2)}) collective-permute-start(bf16[256,1024]{1,0:T(8,128)(2,1)S(1)} %add_convert_fusion.19), channel_id=1, source_target_pairs={{0,8},{8,0},{16,24},{24,16},{1,9},{9,1},{17,25},{25,17},{2,10},{10... | collective-permute-start | bytes 1572872 | tf_op jit(solution)/shard_map/ppermute | solution.py:302
  328.7 12.2 %collective-permute-start.35 = (bf16[256,1024]{1,0:T(8,128)(2,1)S(1)}, bf16[256,1024]{1,0:T(8,128)(2,1)S(1)}, u32[]{:S(2)}, u32[]{:S(2)}) collective-permute-start(bf16[256,1024]{1,0:T(8,128)(2,1)S(1)} %add_convert_fusion.16), channel_id=1, source_target_pairs={{0,16},{8,24},{16,0},{24,8},{1,17},{9,25},{17,1},{25,9},{2,18},{10... | collective-permute-start | bytes 1572872 | tf_op jit(solution)/shard_map/ppermute | solution.py:302
  330.4 11.4 %collective-permute-start.25 = (bf16[256,1024]{1,0:T(8,128)(2,1)S(1)}, bf16[256,1024]{1,0:T(8,128)(2,1)S(1)}, u32[]{:S(2)}, u32[]{:S(2)}) collective-permute-start(bf16[256,1024]{1,0:T(8,128)(2,1)S(1)} %constant_dynamic-slice_fusion.6), channel_id=1, source_target_pairs={{0,1},{1,0},{2,3},{3,2},{4,5},{5,4},{6,7},{7,6},{8,9},{9,8},{10,11... | collective-permute-start | bytes 1572872 | tf_op jit(solution)/shard_map/ppermute | solution.py:302
  339.1 14.8 %collective-permute-start.42 = (bf16[1024,256]{1,0:T(8,128)(2,1)S(1)}, bf16[1024,256]{1,0:T(8,128)(2,1)S(1)}, u32[]{:S(2)}, u32[]{:S(2)}) collective-permute-start(bf16[1024,256]{1,0:T(8,128)(2,1)S(1)} %pad_maximum_fusion.14), channel_id=1, source_target_pairs={{0,2},{2,0},{4,6},{6,4},{1,3},{3,1},{5,7},{7,5},{8,10},{10,8},{12,... | collective-permute-start | bytes 1572872 | tf_op jit(solution)/shard_map/ppermute | solution.py:302
  341.3 27.7 %collective-permute-start.36 = (bf16[256,1024]{1,0:T(8,128)(2,1)S(1)}, bf16[256,1024]{1,0:T(8,128)(2,1)S(1)}, u32[]{:S(2)}, u32[]{:S(2)}) collective-permute-start(bf16[256,1024]{1,0:T(8,128)(2,1)S(1)} %pad_maximum_fusion.13), channel_id=1, source_target_pairs={{0,2},{2,0},{4,6},{6,4},{1,3},{3,1},{5,7},{7,5},{8,10},{10,8},{12,... | collective-permute-start | bytes 1572872 | tf_op jit(solution)/shard_map/ppermute | solution.py:302
  354.0 19.4 %collective-permute-start.43 = (bf16[512,256]{1,0:T(8,128)(2,1)S(1)}, bf16[512,256]{1,0:T(8,128)(2,1)S(1)}, u32[]{:S(2)}, u32[]{:S(2)}) collective-permute-start(bf16[512,256]{1,0:T(8,128)(2,1)S(1)} %slice.422), channel_id=1, source_target_pairs={{0,4},{2,6},{4,0},{6,2},{1,5},{3,7},{5,1},{7,3},{8,12},{10,14},{12... | collective-permute-start | bytes 786440 | tf_op jit(solution)/shard_map/ppermute | solution.py:302
  369.2 13.2 %collective-permute-start.37 = (bf16[256,512]{1,0:T(8,128)(2,1)S(1)}, bf16[256,512]{1,0:T(8,128)(2,1)S(1)}, u32[]{:S(2)}, u32[]{:S(2)}) collective-permute-start(bf16[256,512]{1,0:T(8,128)(2,1)S(1)} %slice.408), channel_id=1, source_target_pairs={{0,4},{2,6},{4,0},{6,2},{1,5},{3,7},{5,1},{7,3},{8,12},{10,14},{12... | collective-permute-start | bytes 786440 | tf_op jit(solution)/shard_map/ppermute | solution.py:302
  370.4 12.7 %collective-permute-start.27 = (bf16[272,1024]{1,0:T(8,128)(2,1)S(1)}, bf16[272,1024]{1,0:T(8,128)(2,1)S(1)}, u32[]{:S(2)}, u32[]{:S(2)}) collective-permute-start(bf16[272,1024]{1,0:T(8,128)(2,1)S(1)} %add_convert_fusion.5), channel_id=1, source_target_pairs={{0,8},{8,0},{16,24},{24,16},{1,9},{9,1},{17,25},{25,17},{2,10},{10... | collective-permute-start | bytes 1671176 | tf_op jit(solution)/shard_map/ppermute | solution.py:302
  371.8 12.4 %collective-permute-start.29 = (bf16[272,1024]{1,0:T(8,128)(2,1)S(1)}, bf16[272,1024]{1,0:T(8,128)(2,1)S(1)}, u32[]{:S(2)}, u32[]{:S(2)}) collective-permute-start(bf16[272,1024]{1,0:T(8,128)(2,1)S(1)} %add_convert_fusion.2), channel_id=1, source_target_pairs={{0,16},{8,24},{16,0},{24,8},{1,17},{9,25},{17,1},{25,9},{2,18},{10... | collective-permute-start | bytes 1671176 | tf_op jit(solution)/shard_map/ppermute | solution.py:302
  384.7 13.0 %collective-permute-start.30 = (bf16[272,1024]{1,0:T(8,128)(2,1)S(1)}, bf16[272,1024]{1,0:T(8,128)(2,1)S(1)}, u32[]{:S(2)}, u32[]{:S(2)}) collective-permute-start(bf16[272,1024]{1,0:T(8,128)(2,1)S(1)} %pad_maximum_fusion.4), channel_id=1, source_target_pairs={{0,2},{2,0},{4,6},{6,4},{1,3},{3,1},{5,7},{7,5},{8,10},{10,8},{12,... | collective-permute-start | bytes 1671176 | tf_op jit(solution)/shard_map/ppermute | solution.py:302
  398.0 12.4 %collective-permute-start.31 = (bf16[272,512]{1,0:T(8,128)(2,1)S(1)}, bf16[272,512]{1,0:T(8,128)(2,1)S(1)}, u32[]{:S(2)}, u32[]{:S(2)}) collective-permute-start(bf16[272,512]{1,0:T(8,128)(2,1)S(1)} %get-tuple-element.124), channel_id=1, source_target_pairs={{0,4},{2,6},{4,0},{6,2},{1,5},{3,7},{5,1},{7,3},{8,12},{10,14},{12... | collective-permute-start | bytes 835592 | tf_op jit(solution)/shard_map/ppermute | solution.py:302
  (79 other events, 586.0 us)
